TPU v7x, 512 devices: a whole 4x4x16 slice. The times are simulated.
512 devices in a mesh: gx: 16 (over z_hi, y, core), gy: 32 (over z_lo, x).
Axes of the slice: x: 4, y: 4, z: 16 (z_hi: 2, z_lo: 8; z = z_hi * 8 + z_lo), core: 2. Of those that a mesh axis runs over, the one named last changes fastest.
Arguments:
- adjoint_in: float32 [19, 256, 4, 4096], P(None, 'gx', None, 'gy'), may hold values from -6 to 6
- velocity: bfloat16 [2, 3, 256, 4, 4096], P(None, None, 'gx', None, 'gy')
- solid_tiles: int32 [64, 4, 1024], P('gx', None, 'gy'), may hold values from 0 to 1, as said below
- link_blocked: int32 [18, 256, 4, 4096], P(None, 'gx', None, 'gy'), may hold values from 0 to 1, as said below
Outputs:
- adjoint_out: float32 [19, 256, 4, 4096], P(None, 'gx', None, 'gy')
- drag_sens: float32 [1], replicated
Inputs may be any that keep to these rules, and one draw needn't show every extreme that they name: `solid_tiles`: 1 on the levels below a tile's building height, heights 0 to 3 per tile. `link_blocked`: entry i - 1 is 1 exactly where the cell x + c_i (periodic in the plane) is solid or lies outside the 4 levels.
All inputs are finite; a program needn't handle non-finite values.
Results may differ from a plain program's by a relative error of at most 0.0003.
Values sent between devices are 32-bit elements; how exact they have to be, the bound alone decides.
A program may use at most 64 MiB of HBM per device.

v0:
```python
import math

import jax
import jax.numpy as jnp
from jax import lax
from jax.sharding import PartitionSpec as P

TILE = 4
STEPS = 2


lattice_speeds = (
    (0, 0, 0),
    (1, 0, 0),
    (-1, 0, 0),
    (0, 1, 0),
    (0, -1, 0),
    (0, 0, 1),
    (0, 0, -1),
    (1, 1, 0),
    (-1, -1, 0),
    (1, -1, 0),
    (-1, 1, 0),
    (1, 0, 1),
    (-1, 0, -1),
    (1, 0, -1),
    (-1, 0, 1),
    (0, 1, 1),
    (0, -1, -1),
    (0, 1, -1),
    (0, -1, 1),
)
lattice_weights = (1.0 / 3.0,) + (1.0 / 18.0,) * 6 + (1.0 / 36.0,) * 12
relax_rate = 1.6
drag_factor = 20.0


def with_halo(block, sides, width):
    for axis, dim in sides:
        count = lax.axis_size(axis)
        forward = [(i, i + 1) for i in range(count - 1)]
        forward.append((count - 1, 0))
        backward = [(target, source) for source, target in forward]
        low = lax.ppermute(
            lax.slice_in_dim(block, block.shape[dim] - width, None, axis=dim), axis, forward
        )
        high = lax.ppermute(lax.slice_in_dim(block, 0, width, axis=dim), axis, backward)
        block = jnp.concatenate([low, block, high], axis=dim)
    return block


def opposite_of(number):
    return number + 1 if number % 2 == 1 else number - 1


def shift_level(field, lift):
    if lift == 1:
        return jnp.concatenate([field[:, 1:], jnp.zeros_like(field[:, :1])], axis=1)
    if lift == -1:
        return jnp.concatenate([jnp.zeros_like(field[:, :1]), field[:, :-1]], axis=1)
    return field


def adjoint_collide(moved, flow, fluid):
    speed_sq = flow[0] * flow[0] + flow[1] * flow[1] + flow[2] * flow[2]
    scalar_part = jnp.zeros_like(speed_sq)
    vector_part = [jnp.zeros_like(speed_sq) for axis_number in range(3)]
    drag_local = jnp.zeros_like(speed_sq)
    for number in range(19):
        speed = lattice_speeds[number]
        along = speed[0] * flow[0] + speed[1] * flow[1] + speed[2] * flow[2]
        weighted = lattice_weights[number] * moved[number]
        scalar_part = scalar_part + weighted * (
            1.0 + 3.0 * along + 4.5 * along * along - 1.5 * speed_sq
        )
        for axis_number in range(3):
            vector_part[axis_number] = vector_part[axis_number] + weighted * (
                3.0 * speed[axis_number]
                + 9.0 * along * speed[axis_number]
                - 3.0 * flow[axis_number]
            )
        drag_local = drag_local + 3.0 * weighted * along
    results = []
    for number in range(19):
        speed = lattice_speeds[number]
        projected = scalar_part
        for axis_number in range(3):
            projected = projected + vector_part[axis_number] * (
                speed[axis_number] - flow[axis_number]
            )
        results.append(fluid * ((1.0 - relax_rate) * moved[number] + relax_rate * projected))
    return (jnp.stack(results), fluid * drag_local)


def stream_back(padded, centre, blocked, span_x, span_y):
    moved = [centre[0]]
    for number in range(1, 19):
        speed = lattice_speeds[number]
        source = padded[
            number, 1 + speed[0] : 1 + speed[0] + span_x, :, 1 + speed[1] : 1 + speed[1] + span_y
        ]
        source = shift_level(source, speed[2])
        bounced = centre[opposite_of(number)] + 2.0 * speed[0]
        moved.append(jnp.where(blocked[number - 1] == 1, bounced, source))
    return moved


def per_device(adjoint_in, velocity, solid_tiles, link_blocked):
    rows_x = adjoint_in.shape[1]
    rows_y = adjoint_in.shape[3]
    levels = adjoint_in.shape[2]
    solid = jnp.repeat(jnp.repeat(solid_tiles, TILE, axis=0), TILE, axis=2)
    fluid = 1.0 - solid.astype(jnp.float32)
    state = adjoint_in
    step_terms = []
    for adjoint_step in range(STEPS):
        flow = velocity[adjoint_step].astype(jnp.float32)
        padded = with_halo(state, (("gx", 1), ("gy", 3)), 1)
        moved = stream_back(padded, state, link_blocked, rows_x, rows_y)
        state, drag_field = adjoint_collide(moved, flow, fluid)
        step_terms.append(jnp.sum(drag_field))
    total = jnp.zeros((), jnp.float32)
    for adjoint_step in range(STEPS):
        total = total + lax.psum(step_terms[adjoint_step], ("gx", "gy"))
    cell_count = rows_x * lax.axis_size("gx") * rows_y * lax.axis_size("gy") * levels
    scale = drag_factor / math.sqrt(cell_count)
    return (state, (-scale * total).reshape(1))


def solution(mesh):
    placed = (
        P(None, "gx", None, "gy"),
        P(None, None, "gx", None, "gy"),
        P("gx", None, "gy"),
        P(None, "gx", None, "gy"),
    )
    return jax.shard_map(
        per_device,
        mesh=mesh,
        in_specs=placed,
        out_specs=(P(None, "gx", None, "gy"), P()),
        check_vma=False,
    )
```

profile of v0, /device:TPU:1, one launch (start us, length us, event | category | flops | bytes accessed | tf_op | source)
XLA Modules:
  0.0 222.9 jit_solution(16425646416944457608)
XLA Ops:
  0.6 0.8 fusion.265
  1.4 4.6 %collective-permute-start.1 = (f32[19,1,4,128]{3,2,1,0:T(4,128)S(1)}, f32[19,1,4,128]{3,2,1,0:T(4,128)S(1)}, u32[]{:S(2)}, u32[]{:S(2)}) collective-permute-start(f32[19,1,4,128]{3,2,1,0:T(4,128)S(1)} %get-tuple-element.193), channel_id=1, source_target_pairs={{0,32},{32,64},{64,96},{96,128},{128,160},{160,192},{192,224},{224... | collective-permute-start | bytes 116744 | tf_op jit(solution)/shard_map/ppermute | solution.py:44
  6.0 6.2 %collective-permute-start = (f32[19,1,4,128]{3,2,1,0:T(4,128)S(1)}, f32[19,1,4,128]{3,2,1,0:T(4,128)S(1)}, u32[]{:S(2)}, u32[]{:S(2)}) collective-permute-start(f32[19,1,4,128]{3,2,1,0:T(4,128)S(1)} %get-tuple-element.194), channel_id=1, source_target_pairs={{32,0},{64,32},{96,64},{128,96},{160,128},{192,160},{224,192},{256... | collective-permute-start | bytes 116744 | tf_op jit(solution)/shard_map/ppermute | solution.py:47
  12.3 1.7 fusion.264
  14.1 0.8 fusion.266
  15.0 0.6 copy-done.67
  15.8 0.1 copy.506
  15.9 0.6 slice.360
  16.5 0.6 slice.361
  17.1 0.4 constant_dynamic-update-slice_fusion.5
  17.6 0.6 fusion.262
  18.3 0.6 fusion.261
  18.9 0.4 fusion.260
  19.3 0.5 copy.541
  19.9 0.5 copy.538
  20.4 10.9 %collective-permute-start.2 = (f32[19,18,4,1]{0,2,3,1:T(4,128)S(1)}, f32[19,18,4,1]{0,2,3,1:T(4,128)}, u32[]{:S(2)}, u32[]{:S(2)}) collective-permute-start(f32[19,18,4,1]{0,2,3,1:T(4,128)S(1)} %copy.538), channel_id=1, source_target_pairs={{1,0},{2,1},{3,2},{4,3},{5,4},{6,5},{7,6},{8,7},{9,8},{10,9},{11,1... | collective-permute-start | bytes 16424 | tf_op jit(solution)/shard_map/ppermute | solution.py:47
  31.3 1.9 collective-permute-start.3
  33.2 0.1 copy.437
  33.3 0.6 slice.367
  33.9 0.6 slice.363
  34.5 0.6 slice.369
  35.2 0.6 slice.365
  35.8 8.9 %collective-permute-done.3 = f32[19,18,4,1]{0,2,3,1:T(4,128)S(1)} collective-permute-done((f32[19,18,4,1]{0,2,3,1:T(4,128)S(1)}, f32[19,18,4,1]{0,2,3,1:T(4,128)S(1)}, u32[]{:S(2)}, u32[]{:S(2)}) %collective-permute-start.3) | collective-permute-done | bytes 5504 | tf_op jit(solution)/shard_map/ppermute | solution.py:44
  44.7 1.0 copy.442
  45.7 1.8 copy.438
  47.8 0.1 fusion.162
  48.0 0.3 copy-done.11
  48.9 1.7 multiply_reduce_fusion.1
  50.6 0.6 constant_dynamic-update-slice_fusion.25
  51.4 0.6 constant_dynamic-update-slice_fusion.17
  52.0 0.6 constant_dynamic-update-slice_fusion.16
  52.6 0.6 constant_dynamic-update-slice_fusion.15
  53.2 0.6 constant_dynamic-update-slice_fusion.14
  53.9 0.6 constant_dynamic-update-slice_fusion.13
  54.5 0.6 constant_dynamic-update-slice_fusion.12
  55.1 0.6 constant_dynamic-update-slice_fusion.11
  55.8 0.6 constant_dynamic-update-slice_fusion.10
  56.4 0.6 constant_dynamic-update-slice_fusion.9
  57.0 0.6 constant_dynamic-update-slice_fusion.8
  57.6 0.6 constant_dynamic-update-slice_fusion.7
  58.3 14.7 %collective-permute-start.4 = (f32[19,1,4,128]{3,2,1,0:T(4,128)S(1)}, f32[19,1,4,128]{3,2,1,0:T(4,128)S(1)}, u32[]{:S(2)}, u32[]{:S(2)}) collective-permute-start(f32[19,1,4,128]{3,2,1,0:T(4,128)S(1)} %bitcast.557), channel_id=1, source_target_pairs={{32,0},{64,32},{96,64},{128,96},{160,128},{192,160},{224,192},{256... | collective-permute-start | bytes 116744 | tf_op jit(solution)/shard_map/ppermute | solution.py:47
  73.0 1.9 collective-permute-start.5
  75.0 0.6 slice.382
  75.6 0.6 slice.381
  76.2 6.9 %collective-permute-done.5 = f32[19,1,4,128]{3,2,1,0:T(4,128)S(1)} collective-permute-done((f32[19,1,4,128]{3,2,1,0:T(4,128)S(1)}, f32[19,1,4,128]{3,2,1,0:T(4,128)S(1)}, u32[]{:S(2)}, u32[]{:S(2)}) %collective-permute-start.5) | collective-permute-done | bytes 38944 | tf_op jit(solution)/shard_map/ppermute | solution.py:44
  83.1 0.2 pad_maximum_fusion
  83.3 0.3 fusion.259
  83.6 0.6 copy.504
  84.2 0.6 copy.502
  84.8 3.1 %collective-permute-start.6 = (f32[19,18,4,1]{0,2,3,1:T(4,128)S(1)}, f32[19,18,4,1]{0,2,3,1:T(4,128)S(1)}, u32[]{:S(2)}, u32[]{:S(2)}) collective-permute-start(f32[19,18,4,1]{0,2,3,1:T(4,128)S(1)} %copy.502), channel_id=1, source_target_pairs={{1,0},{2,1},{3,2},{4,3},{5,4},{6,5},{7,6},{8,7},{9,8},{10,9},{11,1... | collective-permute-start | bytes 16424 | tf_op jit(solution)/shard_map/ppermute | solution.py:47
  87.9 2.1 collective-permute-start.7
  90.1 0.6 slice.385
  90.7 0.6 slice.383
  91.3 0.6 slice.386
  91.9 9.4 %collective-permute-done.7 = f32[19,18,4,1]{0,2,3,1:T(4,128)S(1)} collective-permute-done((f32[19,18,4,1]{0,2,3,1:T(4,128)S(1)}, f32[19,18,4,1]{0,2,3,1:T(4,128)S(1)}, u32[]{:S(2)}, u32[]{:S(2)}) %collective-permute-start.7) | collective-permute-done | bytes 5504 | tf_op jit(solution)/shard_map/ppermute | solution.py:44
  101.3 1.0 copy.505
  102.4 1.1 copy.503
  103.7 0.1 fusion.150
  104.0 0.2 copy-done.32
  104.5 0.1 copy-done.31
  104.8 1.6 multiply_reduce_fusion
  107.7 111.4 %psum.16 = f32[]{:T(128)} all-reduce(f32[]{:T(128)S(6)} %add.2107), channel_id=1, replica_groups=mesh['gx'=16,'gy'=32] {'gx','gy'}, use_global_device_ids=true, to_apply=%region_1.2 | all-reduce | flops 1 | bytes 8 | tf_op jit(solution)/shard_map/psum | solution.py:124
  219.1 0.6 constant_dynamic-update-slice_fusion.44
  220.1 1.1 copy.527
  (185 shorter events, 1.9 us)
Async XLA Ops:
  1.4 15.7 %collective-permute-start.1 = (f32[19,1,4,128]{3,2,1,0:T(4,128)S(1)}, f32[19,1,4,128]{3,2,1,0:T(4,128)S(1)}, u32[]{:S(2)}, u32[]{:S(2)}) collective-permute-start(f32[19,1,4,128]{3,2,1,0:T(4,128)S(1)} %get-tuple-element.193), channel_id=1, source_target_pairs={{0,32},{32,64},{64,96},{96,128},{128,160},{160,192},{192,224},{224... | collective-permute-start | bytes 116744 | tf_op jit(solution)/shard_map/ppermute | solution.py:44
  6.0 8.0 %copy-start.48 = (bf16[2,3,16,4,128]{4,3,2,1,0:T(4,128)(2,1)S(1)}, bf16[2,3,16,4,128]{4,3,2,1,0:T(4,128)(2,1)}, u32[]{:S(2)}) copy-start(bf16[2,3,16,4,128]{4,3,2,1,0:T(4,128)(2,1)} %param.5) | copy-start | bytes 294916
  6.0 8.1 %copy-start.1 = (s32[18,16,4,128]{3,2,1,0:T(4,128)S(1)}, s32[18,16,4,128]{3,2,1,0:T(4,128)}, u32[]{:S(2)}) copy-start(s32[18,16,4,128]{3,2,1,0:T(4,128)} %param.7) | copy-start | bytes 1769476
  6.0 11.5 %collective-permute-start = (f32[19,1,4,128]{3,2,1,0:T(4,128)S(1)}, f32[19,1,4,128]{3,2,1,0:T(4,128)S(1)}, u32[]{:S(2)}, u32[]{:S(2)}) collective-permute-start(f32[19,1,4,128]{3,2,1,0:T(4,128)S(1)} %get-tuple-element.194), channel_id=1, source_target_pairs={{32,0},{64,32},{96,64},{128,96},{160,128},{192,160},{224,192},{256... | collective-permute-start | bytes 116744 | tf_op jit(solution)/shard_map/ppermute | solution.py:47
  15.0 2.2 copy-start
  20.4 25.3 %collective-permute-start.2 = (f32[19,18,4,1]{0,2,3,1:T(4,128)S(1)}, f32[19,18,4,1]{0,2,3,1:T(4,128)}, u32[]{:S(2)}, u32[]{:S(2)}) collective-permute-start(f32[19,18,4,1]{0,2,3,1:T(4,128)S(1)} %copy.538), channel_id=1, source_target_pairs={{1,0},{2,1},{3,2},{4,3},{5,4},{6,5},{7,6},{8,7},{9,8},{10,9},{11,1... | collective-permute-start | bytes 16424 | tf_op jit(solution)/shard_map/ppermute | solution.py:47
  31.3 13.4 %collective-permute-start.3 = (f32[19,18,4,1]{0,2,3,1:T(4,128)S(1)}, f32[19,18,4,1]{0,2,3,1:T(4,128)S(1)}, u32[]{:S(2)}, u32[]{:S(2)}) collective-permute-start(f32[19,18,4,1]{0,2,3,1:T(4,128)S(1)} %copy.541), channel_id=1, source_target_pairs={{0,1},{1,2},{2,3},{3,4},{4,5},{5,6},{6,7},{7,8},{8,9},{9,10},{10,1... | collective-permute-start | bytes 16424 | tf_op jit(solution)/shard_map/ppermute | solution.py:44
  47.6 0.8 copy-start.13
  47.6 0.8 copy-start.14
  47.6 0.8 copy-start.15
  47.6 0.8 copy-start.16
  47.6 0.8 copy-start.17
  47.6 0.8 copy-start.18
  47.7 0.8 copy-start.19
  47.7 0.8 copy-start.20
  47.7 0.9 copy-start.21
  47.7 0.9 copy-start.22
  47.7 0.9 copy-start.23
  47.7 0.9 copy-start.35
  47.7 0.9 copy-start.36
  47.7 0.9 copy-start.37
  47.7 0.9 copy-start.38
  47.7 0.9 copy-start.41
  47.8 0.9 copy-start.42
  47.8 0.9 copy-start.43
  47.8 0.9 copy-start.45
  47.9 0.8 copy-start.9
  47.9 0.8 copy-start.10
  47.9 0.8 copy-start.8
  48.0 0.8 copy-start.6
  48.0 0.8 copy-start.7
  48.0 0.8 copy-start.4
  48.0 0.8 copy-start.2
  48.0 0.8 copy-start.3
  58.3 17.9 %collective-permute-start.4 = (f32[19,1,4,128]{3,2,1,0:T(4,128)S(1)}, f32[19,1,4,128]{3,2,1,0:T(4,128)S(1)}, u32[]{:S(2)}, u32[]{:S(2)}) collective-permute-start(f32[19,1,4,128]{3,2,1,0:T(4,128)S(1)} %bitcast.557), channel_id=1, source_target_pairs={{32,0},{64,32},{96,64},{128,96},{160,128},{192,160},{224,192},{256... | collective-permute-start | bytes 116744 | tf_op jit(solution)/shard_map/ppermute | solution.py:47
  73.0 10.1 %collective-permute-start.5 = (f32[19,1,4,128]{3,2,1,0:T(4,128)S(1)}, f32[19,1,4,128]{3,2,1,0:T(4,128)S(1)}, u32[]{:S(2)}, u32[]{:S(2)}) collective-permute-start(f32[19,1,4,128]{3,2,1,0:T(4,128)S(1)} %bitcast.556), channel_id=1, source_target_pairs={{0,32},{32,64},{64,96},{96,128},{128,160},{160,192},{192,224},{224... | collective-permute-start | bytes 116744 | tf_op jit(solution)/shard_map/ppermute | solution.py:44
  84.8 17.6 %collective-permute-start.6 = (f32[19,18,4,1]{0,2,3,1:T(4,128)S(1)}, f32[19,18,4,1]{0,2,3,1:T(4,128)S(1)}, u32[]{:S(2)}, u32[]{:S(2)}) collective-permute-start(f32[19,18,4,1]{0,2,3,1:T(4,128)S(1)} %copy.502), channel_id=1, source_target_pairs={{1,0},{2,1},{3,2},{4,3},{5,4},{6,5},{7,6},{8,7},{9,8},{10,9},{11,1... | collective-permute-start | bytes 16424 | tf_op jit(solution)/shard_map/ppermute | solution.py:47
  87.9 13.4 %collective-permute-start.7 = (f32[19,18,4,1]{0,2,3,1:T(4,128)S(1)}, f32[19,18,4,1]{0,2,3,1:T(4,128)S(1)}, u32[]{:S(2)}, u32[]{:S(2)}) collective-permute-start(f32[19,18,4,1]{0,2,3,1:T(4,128)S(1)} %copy.504), channel_id=1, source_target_pairs={{0,1},{1,2},{2,3},{3,4},{4,5},{5,6},{6,7},{7,8},{8,9},{9,10},{10,1... | collective-permute-start | bytes 16424 | tf_op jit(solution)/shard_map/ppermute | solution.py:44
  103.4 0.8 copy-start.33
  103.5 0.8 copy-start.47
  103.5 0.8 copy-start.49
  103.5 0.8 copy-start.53
  103.5 0.8 copy-start.54
  103.6 0.8 copy-start.55
  103.6 0.8 copy-start.56
  103.6 0.8 copy-start.57
  103.6 0.8 copy-start.58
  103.6 0.8 copy-start.59
  103.6 0.8 copy-start.60
  103.6 0.8 copy-start.61
  103.6 0.8 copy-start.62
  103.6 0.8 copy-start.63
  103.6 0.8 copy-start.64
  103.7 0.8 copy-start.65
  103.7 0.8 copy-start.66
  103.9 0.8 copy-start.29
  103.9 0.8 copy-start.30
  103.9 0.8 copy-start.28
  103.9 0.8 copy-start.26
  103.9 0.8 copy-start.27
  103.9 0.8 copy-start.25
  104.0 0.8 copy-start.5
  104.0 0.8 copy-start.24
  106.4 112.7 %copy-start.34 = (f32[16,4,128]{2,0,1:T(8,128)S(1)}, f32[16,4,128]{2,0,1:T(8,128)}, u32[]{:S(2)}) copy-start(f32[16,4,128]{2,0,1:T(8,128)} %get-tuple-element.15) | copy-start | bytes 98308
  (12 other events, 9.2 us)
where the time goes:
time: 224 us; the launch traced here: 223 us
  blocking collectives  111 us (50%)
  starting transfers between devices  45.5 us (20%)
  waiting for transfers between devices  25.3 us (11%)
  local copies, waits for them, and re-layouts  23.7 us (11%)
  other arithmetic  12.3 us (5%)
  between operations  4.66 us (2%)
    psum x1, blocking collectives, per_device(): total = total + lax.psum(step_terms[adjoint_step], ('gx', 'gy'))  111 us
    ppermute x4, starting transfers between devices, with_halo(): lax.ppermute(lax.slice_in_dim(block, 0, width, axis=dim), axis, backward)  35 us
    ppermute x4, waiting for transfers between devices, with_halo(): lax.ppermute(lax.slice_in_dim(block, block.shape[dim] - width, None, axis...  25.3 us
    ppermute x4, starting transfers between devices, with_halo(): lax.ppermute(lax.slice_in_dim(block, block.shape[dim] - width, None, axis...  10.6 us
    unnamed x36, other arithmetic  7.93 us
    unnamed x141, local copies, waits for them, and re-layouts  5 us
  transfers between devices with their start and end apart: 8, of which 3 were waited for; matrix products, arithmetic and copies ran while one was open for 5% of the time, Pallas kernels for 0%

commit v1 on v0

--- a/solution.py
+++ b/solution.py
@@ -1,9 +1,14 @@
+import functools
 import math
 
 import jax
 import jax.numpy as jnp
 from jax import lax
+from jax.experimental import pallas as pl
+from jax.experimental.pallas import tpu as pltpu
 from jax.sharding import PartitionSpec as P
+
+MESH = pl.DeviceIdType.MESH
 
 TILE = 4
 STEPS = 2
@@ -105,6 +110,84 @@
     return moved
 
 
+def sum_kernel(nx, ny, part_ref, out_ref, row_buf, col_buf, row_sum, send_a, recv_a, send_b, recv_b):
+    me_x = lax.axis_index("gx")
+    me_y = lax.axis_index("gy")
+    barrier = pltpu.get_barrier_semaphore()
+    for k in range(1, ny):
+        peer = lax.rem(me_y + k, ny)
+        pl.semaphore_signal(barrier, inc=1, device_id=(me_x, peer), device_id_type=MESH)
+    for k in range(1, nx):
+        peer = lax.rem(me_x + k, nx)
+        pl.semaphore_signal(barrier, inc=1, device_id=(peer, me_y), device_id_type=MESH)
+    pl.semaphore_wait(barrier, nx + ny - 2)
+
+    row_copies = []
+    for k in range(1, ny):
+        peer = lax.rem(me_y + k, ny)
+        copy = pltpu.make_async_remote_copy(
+            src_ref=part_ref,
+            dst_ref=row_buf.at[me_y],
+            send_sem=send_a.at[k],
+            recv_sem=recv_a.at[k],
+            device_id=(me_x, peer),
+            device_id_type=MESH,
+        )
+        copy.start()
+        row_copies.append(copy)
+    row_buf[me_y] = part_ref[...]
+    for copy in row_copies:
+        copy.wait()
+    total = row_buf[0]
+    for j in range(1, ny):
+        total = total + row_buf[j]
+    row_sum[...] = total
+
+    col_copies = []
+    for k in range(1, nx):
+        peer = lax.rem(me_x + k, nx)
+        copy = pltpu.make_async_remote_copy(
+            src_ref=row_sum,
+            dst_ref=col_buf.at[me_x],
+            send_sem=send_b.at[k],
+            recv_sem=recv_b.at[k],
+            device_id=(peer, me_y),
+            device_id_type=MESH,
+        )
+        copy.start()
+        col_copies.append(copy)
+    col_buf[me_x] = total
+    for copy in col_copies:
+        copy.wait()
+    total = col_buf[0]
+    for j in range(1, nx):
+        total = total + col_buf[j]
+    out_ref[...] = total
+
+
+def mesh_sum(value):
+    nx = lax.axis_size("gx")
+    ny = lax.axis_size("gy")
+    part = jnp.broadcast_to(value, (8, 128)).astype(jnp.float32)
+    out = pl.pallas_call(
+        functools.partial(sum_kernel, nx, ny),
+        out_shape=jax.ShapeDtypeStruct((8, 128), jnp.float32),
+        in_specs=[pl.BlockSpec(memory_space=pltpu.VMEM)],
+        out_specs=pl.BlockSpec(memory_space=pltpu.VMEM),
+        scratch_shapes=[
+            pltpu.VMEM((ny, 8, 128), jnp.float32),
+            pltpu.VMEM((nx, 8, 128), jnp.float32),
+            pltpu.VMEM((8, 128), jnp.float32),
+            pltpu.SemaphoreType.DMA((ny,)),
+            pltpu.SemaphoreType.DMA((ny,)),
+            pltpu.SemaphoreType.DMA((nx,)),
+            pltpu.SemaphoreType.DMA((nx,)),
+        ],
+        compiler_params=pltpu.CompilerParams(collective_id=0, has_side_effects=True),
+    )(part)
+    return out[0, 0]
+
+
 def per_device(adjoint_in, velocity, solid_tiles, link_blocked):
     rows_x = adjoint_in.shape[1]
     rows_y = adjoint_in.shape[3]
@@ -119,9 +202,10 @@
         moved = stream_back(padded, state, link_blocked, rows_x, rows_y)
         state, drag_field = adjoint_collide(moved, flow, fluid)
         step_terms.append(jnp.sum(drag_field))
-    total = jnp.zeros((), jnp.float32)
-    for adjoint_step in range(STEPS):
-        total = total + lax.psum(step_terms[adjoint_step], ("gx", "gy"))
+    local = step_terms[0]
+    for adjoint_step in range(1, STEPS):
+        local = local + step_terms[adjoint_step]
+    total = mesh_sum(local)
     cell_count = rows_x * lax.axis_size("gx") * rows_y * lax.axis_size("gy") * levels
     scale = drag_factor / math.sqrt(cell_count)
     return (state, (-scale * total).reshape(1))

time: 224 us -> 153 us (0.68)
  blocking collectives: 111 us -> 0 us
  Pallas kernels: 0 us -> 39 us
    psum x1 -> x0, blocking collectives: 111 us -> none  [per_device(): total = total + lax.psum(step_terms[adjoint_step], ('gx', 'gy'))]
    pallas_call x0 -> x1, Pallas kernels: none -> 39 us  [mesh_sum(): pl.pallas_call(functools.partial(sum_kernel, nx, ny), out_shape=jax.Shape...]
  transfers between devices with their start and end apart: 8 -> 8, of which waited for: 3 -> 3; matrix products, arithmetic and copies ran while one was open for 5% -> 8% of each run, Pallas kernels for 0% -> 0%
where the time goes in v1:
time: 153 us; the launch traced here: 152 us
  starting transfers between devices  45.7 us (30%)
  Pallas kernels  39 us (25%)
  local copies, waits for them, and re-layouts  25.4 us (17%)
  waiting for transfers between devices  25.2 us (16%)
  other arithmetic  12.2 us (8%)
  between operations  4.66 us (3%)
    pallas_call x1, Pallas kernels, mesh_sum(): pl.pallas_call(functools.partial(sum_kernel, nx, ny), out_shape=jax.Shape...  39 us
    ppermute x4, starting transfers between devices, with_halo(): lax.ppermute(lax.slice_in_dim(block, 0, width, axis=dim), axis, backward)  35 us
    ppermute x4, waiting for transfers between devices, with_halo(): lax.ppermute(lax.slice_in_dim(block, block.shape[dim] - width, None, axis...  25.2 us
    ppermute x4, starting transfers between devices, with_halo(): lax.ppermute(lax.slice_in_dim(block, block.shape[dim] - width, None, axis...  10.8 us
    unnamed x36, other arithmetic  7.86 us
    unnamed x141, local copies, waits for them, and re-layouts  5 us
    slice x10, local copies, waits for them, and re-layouts, shift_level(): return jnp.concatenate([field[:, 1:], jnp.zeros_like(field[:, :1])], axis=1)  3.65 us
    reduce_sum x2, other arithmetic, per_device(): step_terms.append(jnp.sum(drag_field))  3.28 us
  transfers between devices with their start and end apart: 8, of which 3 were waited for; matrix products, arithmetic and copies ran while one was open for 8% of the time, Pallas kernels for 0%

profile of v1, /device:TPU:1, one launch (start us, length us, event | category | flops | bytes accessed | tf_op | source)
XLA Modules:
  0.0 152.2 jit_solution(7600834934578735686)
XLA Ops:
  0.6 0.8 fusion.265
  1.4 4.6 %collective-permute-start.1 = (f32[19,1,4,128]{3,2,1,0:T(4,128)S(1)}, f32[19,1,4,128]{3,2,1,0:T(4,128)S(1)}, u32[]{:S(2)}, u32[]{:S(2)}) collective-permute-start(f32[19,1,4,128]{3,2,1,0:T(4,128)S(1)} %get-tuple-element.193), channel_id=1, source_target_pairs={{0,32},{32,64},{64,96},{96,128},{128,160},{160,192},{192,224},{224... | collective-permute-start | bytes 116744 | tf_op jit(solution)/shard_map/ppermute | solution.py:49
  6.0 6.2 %collective-permute-start = (f32[19,1,4,128]{3,2,1,0:T(4,128)S(1)}, f32[19,1,4,128]{3,2,1,0:T(4,128)S(1)}, u32[]{:S(2)}, u32[]{:S(2)}) collective-permute-start(f32[19,1,4,128]{3,2,1,0:T(4,128)S(1)} %get-tuple-element.194), channel_id=1, source_target_pairs={{32,0},{64,32},{96,64},{128,96},{160,128},{192,160},{224,192},{256... | collective-permute-start | bytes 116744 | tf_op jit(solution)/shard_map/ppermute | solution.py:52
  12.3 1.7 %fusion.264 = (f32[1,16,4,128]{3,2,1,0:T(4,128)S(1)}, f32[1,16,4,128]{3,2,1,0:T(4,128)S(1)}, f32[1,16,4,128]{3,2,1,0:T(4,128)S(1)}, f32[1,16,4,128]{3,2,1,0:T(4,...) fusion(f32[19,16,4,128]{3,2,1,0:T(4,128)} %param.4), kind=kLoop, calls=%fused_computation.493 | loop fusion | bytes 1245184 | tf_op jit(solution)/shard_map/slice | solution.py:108
  14.1 0.8 fusion.266
  15.0 0.7 copy-done.67
  15.9 0.6 slice.363
  16.5 0.6 slice.364
  17.1 0.4 constant_dynamic-update-slice_fusion.5
  17.6 0.6 fusion.262
  18.2 0.6 fusion.261
  18.8 0.4 fusion.260
  19.3 0.5 copy.541
  19.8 0.5 copy.538
  20.3 10.9 %collective-permute-start.2 = (f32[19,18,4,1]{0,2,3,1:T(4,128)S(1)}, f32[19,18,4,1]{0,2,3,1:T(4,128)}, u32[]{:S(2)}, u32[]{:S(2)}) collective-permute-start(f32[19,18,4,1]{0,2,3,1:T(4,128)S(1)} %copy.538), channel_id=1, source_target_pairs={{1,0},{2,1},{3,2},{4,3},{5,4},{6,5},{7,6},{8,7},{9,8},{10,9},{11,1... | collective-permute-start | bytes 16424 | tf_op jit(solution)/shard_map/ppermute | solution.py:52
  31.2 1.9 %collective-permute-start.3 = (f32[19,18,4,1]{0,2,3,1:T(4,128)S(1)}, f32[19,18,4,1]{0,2,3,1:T(4,128)S(1)}, u32[]{:S(2)}, u32[]{:S(2)}) collective-permute-start(f32[19,18,4,1]{0,2,3,1:T(4,128)S(1)} %copy.541), channel_id=1, source_target_pairs={{0,1},{1,2},{2,3},{3,4},{4,5},{5,6},{6,7},{7,8},{8,9},{9,10},{10,1... | collective-permute-start | bytes 16424 | tf_op jit(solution)/shard_map/ppermute | solution.py:49
  33.3 0.6 slice.370
  33.9 0.6 slice.366
  34.5 0.6 slice.372
  35.1 0.6 slice.368
  35.7 8.9 %collective-permute-done.3 = f32[19,18,4,1]{0,2,3,1:T(4,128)S(1)} collective-permute-done((f32[19,18,4,1]{0,2,3,1:T(4,128)S(1)}, f32[19,18,4,1]{0,2,3,1:T(4,128)S(1)}, u32[]{:S(2)}, u32[]{:S(2)}) %collective-permute-start.3) | collective-permute-done | bytes 5504 | tf_op jit(solution)/shard_map/ppermute | solution.py:49
  44.7 1.0 copy.442
  45.7 1.8 %copy.438 = f32[19,18,4,1]{3,1,2,0:T(8,128)S(1)} copy(f32[19,18,4,1]{0,2,3,1:T(4,128)} %collective-permute-done.2) | data formatting | bytes 10944 | tf_op jit(solution)/shard_map/ppermute | solution.py:52
  47.7 0.1 fusion.162
  48.0 0.3 copy-done.11
  48.8 1.7 %multiply_reduce_fusion.1 = (f32[]{:T(128)}, f32[16,4,128]{2,0,1:T(8,128)S(1)}, f32[16,4,128]{2,0,1:T(8,128)S(1)}, pred[16,4,128]{2,0,1:T(8,128)(4,1)}, f32[16,4...) fusion(f32[16,4,128]{2,0,1:T(8,128)S(1)} %copy.506, ...), kind=kLoop, calls=%fused_computation.356 | loop fusion | flops 1171455 | bytes 3136196 | tf_op jit(solution)/shard_map/reduce_sum | solution.py:204
  50.5 0.6 constant_dynamic-update-slice_fusion.25
  51.3 0.6 constant_dynamic-update-slice_fusion.17
  51.9 0.6 constant_dynamic-update-slice_fusion.16
  52.6 0.6 constant_dynamic-update-slice_fusion.15
  53.2 0.6 constant_dynamic-update-slice_fusion.14
  53.8 0.6 constant_dynamic-update-slice_fusion.13
  54.4 0.6 constant_dynamic-update-slice_fusion.12
  55.0 0.6 constant_dynamic-update-slice_fusion.11
  55.7 0.6 constant_dynamic-update-slice_fusion.10
  56.3 0.6 constant_dynamic-update-slice_fusion.9
  56.9 0.6 constant_dynamic-update-slice_fusion.8
  57.5 0.6 constant_dynamic-update-slice_fusion.7
  58.2 14.7 %collective-permute-start.4 = (f32[19,1,4,128]{3,2,1,0:T(4,128)S(1)}, f32[19,1,4,128]{3,2,1,0:T(4,128)S(1)}, u32[]{:S(2)}, u32[]{:S(2)}) collective-permute-start(f32[19,1,4,128]{3,2,1,0:T(4,128)S(1)} %bitcast.557), channel_id=1, source_target_pairs={{32,0},{64,32},{96,64},{128,96},{160,128},{192,160},{224,192},{256... | collective-permute-start | bytes 116744 | tf_op jit(solution)/shard_map/ppermute | solution.py:52
  72.9 1.9 %collective-permute-start.5 = (f32[19,1,4,128]{3,2,1,0:T(4,128)S(1)}, f32[19,1,4,128]{3,2,1,0:T(4,128)S(1)}, u32[]{:S(2)}, u32[]{:S(2)}) collective-permute-start(f32[19,1,4,128]{3,2,1,0:T(4,128)S(1)} %bitcast.556), channel_id=1, source_target_pairs={{0,32},{32,64},{64,96},{96,128},{128,160},{160,192},{192,224},{224... | collective-permute-start | bytes 116744 | tf_op jit(solution)/shard_map/ppermute | solution.py:49
  74.8 0.6 slice.385
  75.4 0.6 slice.384
  76.0 7.0 %collective-permute-done.5 = f32[19,1,4,128]{3,2,1,0:T(4,128)S(1)} collective-permute-done((f32[19,1,4,128]{3,2,1,0:T(4,128)S(1)}, f32[19,1,4,128]{3,2,1,0:T(4,128)S(1)}, u32[]{:S(2)}, u32[]{:S(2)}) %collective-permute-start.5) | collective-permute-done | bytes 38944 | tf_op jit(solution)/shard_map/ppermute | solution.py:49
  83.0 0.2 pad_maximum_fusion
  83.2 0.3 fusion.259
  83.5 0.6 copy.504
  84.1 0.6 copy.502
  84.7 3.1 %collective-permute-start.6 = (f32[19,18,4,1]{0,2,3,1:T(4,128)S(1)}, f32[19,18,4,1]{0,2,3,1:T(4,128)S(1)}, u32[]{:S(2)}, u32[]{:S(2)}) collective-permute-start(f32[19,18,4,1]{0,2,3,1:T(4,128)S(1)} %copy.502), channel_id=1, source_target_pairs={{1,0},{2,1},{3,2},{4,3},{5,4},{6,5},{7,6},{8,7},{9,8},{10,9},{11,1... | collective-permute-start | bytes 16424 | tf_op jit(solution)/shard_map/ppermute | solution.py:52
  87.8 2.3 %collective-permute-start.7 = (f32[19,18,4,1]{0,2,3,1:T(4,128)S(1)}, f32[19,18,4,1]{0,2,3,1:T(4,128)S(1)}, u32[]{:S(2)}, u32[]{:S(2)}) collective-permute-start(f32[19,18,4,1]{0,2,3,1:T(4,128)S(1)} %copy.504), channel_id=1, source_target_pairs={{0,1},{1,2},{2,3},{3,4},{4,5},{5,6},{6,7},{7,8},{8,9},{9,10},{10,1... | collective-permute-start | bytes 16424 | tf_op jit(solution)/shard_map/ppermute | solution.py:49
  90.2 0.6 slice.388
  90.8 0.6 slice.386
  91.4 0.6 slice.389
  92.0 9.2 %collective-permute-done.7 = f32[19,18,4,1]{0,2,3,1:T(4,128)S(1)} collective-permute-done((f32[19,18,4,1]{0,2,3,1:T(4,128)S(1)}, f32[19,18,4,1]{0,2,3,1:T(4,128)S(1)}, u32[]{:S(2)}, u32[]{:S(2)}) %collective-permute-start.7) | collective-permute-done | bytes 5504 | tf_op jit(solution)/shard_map/ppermute | solution.py:49
  101.2 1.0 copy.505
  102.3 1.1 copy.503
  103.6 0.1 fusion.150
  103.9 0.2 copy-done.32
  104.4 0.1 copy-done.31
  104.7 1.6 %multiply_reduce_fusion = (f32[]{:T(128)}, f32[16,4,128]{2,0,1:T(8,128)}, f32[16,4,128]{2,0,1:T(8,128)S(1)}, f32[16,4,128]{2,0,1:T(8,128)S(1)}, f32[16,4,128]{2,...) fusion(f32[16,4,128]{2,0,1:T(8,128)S(1)} %copy.506, ...), kind=kLoop, calls=%fused_computation.355 | loop fusion | flops 1138687 | bytes 2480836 | tf_op jit(solution)/shard_map/reduce_sum | solution.py:204
  107.5 0.6 broadcast_in_dim.11.part_ref
  108.1 39.0 %shard_map.59 = f32[8,128]{1,0:T(8,128)} custom-call(f32[8,128]{1,0:T(8,128)} %broadcast_in_dim.11.part_ref), custom_call_target="tpu_custom_call" | custom-call | tf_op jit(solution)/shard_map/pallas_call | solution.py:172
  147.1 1.2 slice.355
  148.3 0.6 constant_dynamic-update-slice_fusion.44
  149.3 1.1 copy.527
  (187 shorter events, 2.1 us)
Async XLA Ops:
  1.4 15.6 %collective-permute-start.1 = (f32[19,1,4,128]{3,2,1,0:T(4,128)S(1)}, f32[19,1,4,128]{3,2,1,0:T(4,128)S(1)}, u32[]{:S(2)}, u32[]{:S(2)}) collective-permute-start(f32[19,1,4,128]{3,2,1,0:T(4,128)S(1)} %get-tuple-element.193), channel_id=1, source_target_pairs={{0,32},{32,64},{64,96},{96,128},{128,160},{160,192},{192,224},{224... | collective-permute-start | bytes 116744 | tf_op jit(solution)/shard_map/ppermute | solution.py:49
  6.0 8.0 %copy-start.48 = (bf16[2,3,16,4,128]{4,3,2,1,0:T(4,128)(2,1)S(1)}, bf16[2,3,16,4,128]{4,3,2,1,0:T(4,128)(2,1)}, u32[]{:S(2)}) copy-start(bf16[2,3,16,4,128]{4,3,2,1,0:T(4,128)(2,1)} %param.5) | copy-start | bytes 294916
  6.0 8.0 %copy-start.1 = (s32[18,16,4,128]{3,2,1,0:T(4,128)S(1)}, s32[18,16,4,128]{3,2,1,0:T(4,128)}, u32[]{:S(2)}) copy-start(s32[18,16,4,128]{3,2,1,0:T(4,128)} %param.7) | copy-start | bytes 1769476
  6.0 11.5 %collective-permute-start = (f32[19,1,4,128]{3,2,1,0:T(4,128)S(1)}, f32[19,1,4,128]{3,2,1,0:T(4,128)S(1)}, u32[]{:S(2)}, u32[]{:S(2)}) collective-permute-start(f32[19,1,4,128]{3,2,1,0:T(4,128)S(1)} %get-tuple-element.194), channel_id=1, source_target_pairs={{32,0},{64,32},{96,64},{128,96},{160,128},{192,160},{224,192},{256... | collective-permute-start | bytes 116744 | tf_op jit(solution)/shard_map/ppermute | solution.py:52
  14.9 2.2 %copy-start = (f32[19,16,4,128]{3,2,1,0:T(4,128)S(1)}, f32[19,16,4,128]{3,2,1,0:T(4,128)}, u32[]{:S(2)}) copy-start(f32[19,16,4,128]{3,2,1,0:T(4,128)} %param.4) | copy-start | bytes 1867780
  20.3 25.3 %collective-permute-start.2 = (f32[19,18,4,1]{0,2,3,1:T(4,128)S(1)}, f32[19,18,4,1]{0,2,3,1:T(4,128)}, u32[]{:S(2)}, u32[]{:S(2)}) collective-permute-start(f32[19,18,4,1]{0,2,3,1:T(4,128)S(1)} %copy.538), channel_id=1, source_target_pairs={{1,0},{2,1},{3,2},{4,3},{5,4},{6,5},{7,6},{8,7},{9,8},{10,9},{11,1... | collective-permute-start | bytes 16424 | tf_op jit(solution)/shard_map/ppermute | solution.py:52
  31.2 13.4 %collective-permute-start.3 = (f32[19,18,4,1]{0,2,3,1:T(4,128)S(1)}, f32[19,18,4,1]{0,2,3,1:T(4,128)S(1)}, u32[]{:S(2)}, u32[]{:S(2)}) collective-permute-start(f32[19,18,4,1]{0,2,3,1:T(4,128)S(1)} %copy.541), channel_id=1, source_target_pairs={{0,1},{1,2},{2,3},{3,4},{4,5},{5,6},{6,7},{7,8},{8,9},{9,10},{10,1... | collective-permute-start | bytes 16424 | tf_op jit(solution)/shard_map/ppermute | solution.py:49
  47.5 0.8 copy-start.13
  47.6 0.8 copy-start.14
  47.6 0.8 copy-start.15
  47.6 0.8 copy-start.16
  47.6 0.8 copy-start.17
  47.6 0.8 copy-start.18
  47.6 0.8 copy-start.19
  47.6 0.8 copy-start.20
  47.6 0.9 copy-start.21
  47.6 0.9 copy-start.22
  47.6 0.9 copy-start.23
  47.7 0.9 copy-start.35
  47.7 0.9 copy-start.36
  47.7 0.9 copy-start.37
  47.7 0.9 copy-start.38
  47.7 0.9 copy-start.41
  47.7 0.9 copy-start.42
  47.7 0.9 copy-start.43
  47.7 0.9 copy-start.45
  47.9 0.8 copy-start.9
  47.9 0.8 copy-start.10
  47.9 0.8 copy-start.8
  47.9 0.8 copy-start.6
  47.9 0.8 copy-start.7
  48.0 0.8 copy-start.4
  48.0 0.8 copy-start.2
  48.0 0.8 copy-start.3
  58.2 17.9 %collective-permute-start.4 = (f32[19,1,4,128]{3,2,1,0:T(4,128)S(1)}, f32[19,1,4,128]{3,2,1,0:T(4,128)S(1)}, u32[]{:S(2)}, u32[]{:S(2)}) collective-permute-start(f32[19,1,4,128]{3,2,1,0:T(4,128)S(1)} %bitcast.557), channel_id=1, source_target_pairs={{32,0},{64,32},{96,64},{128,96},{160,128},{192,160},{224,192},{256... | collective-permute-start | bytes 116744 | tf_op jit(solution)/shard_map/ppermute | solution.py:52
  72.9 10.1 %collective-permute-start.5 = (f32[19,1,4,128]{3,2,1,0:T(4,128)S(1)}, f32[19,1,4,128]{3,2,1,0:T(4,128)S(1)}, u32[]{:S(2)}, u32[]{:S(2)}) collective-permute-start(f32[19,1,4,128]{3,2,1,0:T(4,128)S(1)} %bitcast.556), channel_id=1, source_target_pairs={{0,32},{32,64},{64,96},{96,128},{128,160},{160,192},{192,224},{224... | collective-permute-start | bytes 116744 | tf_op jit(solution)/shard_map/ppermute | solution.py:49
  84.7 17.6 %collective-permute-start.6 = (f32[19,18,4,1]{0,2,3,1:T(4,128)S(1)}, f32[19,18,4,1]{0,2,3,1:T(4,128)S(1)}, u32[]{:S(2)}, u32[]{:S(2)}) collective-permute-start(f32[19,18,4,1]{0,2,3,1:T(4,128)S(1)} %copy.502), channel_id=1, source_target_pairs={{1,0},{2,1},{3,2},{4,3},{5,4},{6,5},{7,6},{8,7},{9,8},{10,9},{11,1... | collective-permute-start | bytes 16424 | tf_op jit(solution)/shard_map/ppermute | solution.py:52
  87.8 13.4 %collective-permute-start.7 = (f32[19,18,4,1]{0,2,3,1:T(4,128)S(1)}, f32[19,18,4,1]{0,2,3,1:T(4,128)S(1)}, u32[]{:S(2)}, u32[]{:S(2)}) collective-permute-start(f32[19,18,4,1]{0,2,3,1:T(4,128)S(1)} %copy.504), channel_id=1, source_target_pairs={{0,1},{1,2},{2,3},{3,4},{4,5},{5,6},{6,7},{7,8},{8,9},{9,10},{10,1... | collective-permute-start | bytes 16424 | tf_op jit(solution)/shard_map/ppermute | solution.py:49
  103.3 0.8 copy-start.33
  103.4 0.8 copy-start.47
  103.4 0.8 copy-start.49
  103.4 0.8 copy-start.53
  103.4 0.8 copy-start.54
  103.5 0.8 copy-start.55
  103.5 0.8 copy-start.56
  103.5 0.8 copy-start.57
  103.5 0.8 copy-start.58
  103.5 0.8 copy-start.59
  103.5 0.8 copy-start.60
  103.5 0.8 copy-start.61
  103.5 0.8 copy-start.62
  103.5 0.8 copy-start.63
  103.5 0.8 copy-start.64
  103.6 0.8 copy-start.65
  103.6 0.8 copy-start.66
  103.8 0.8 copy-start.29
  103.8 0.8 copy-start.30
  103.8 0.8 copy-start.28
  103.8 0.8 copy-start.26
  103.8 0.8 copy-start.27
  103.8 0.8 copy-start.25
  103.9 0.8 copy-start.5
  103.9 0.8 copy-start.24
  106.2 42.0 %copy-start.34 = (f32[16,4,128]{2,0,1:T(8,128)S(1)}, f32[16,4,128]{2,0,1:T(8,128)}, u32[]{:S(2)}) copy-start(f32[16,4,128]{2,0,1:T(8,128)} %get-tuple-element.15) | copy-start | bytes 98308
  (12 other events, 9.2 us)

commit v2 on v1

v2 whole, which is shorter than its diff:
```python
import functools
import math

import jax
import jax.numpy as jnp
from jax import lax
from jax.experimental import pallas as pl
from jax.experimental.pallas import tpu as pltpu
from jax.sharding import PartitionSpec as P

MESH = pl.DeviceIdType.MESH
TILE = 4
STEPS = 2

lattice_speeds = (
    (0, 0, 0),
    (1, 0, 0),
    (-1, 0, 0),
    (0, 1, 0),
    (0, -1, 0),
    (0, 0, 1),
    (0, 0, -1),
    (1, 1, 0),
    (-1, -1, 0),
    (1, -1, 0),
    (-1, 1, 0),
    (1, 0, 1),
    (-1, 0, -1),
    (1, 0, -1),
    (-1, 0, 1),
    (0, 1, 1),
    (0, -1, -1),
    (0, 1, -1),
    (0, -1, 1),
)
lattice_weights = (1.0 / 3.0,) + (1.0 / 18.0,) * 6 + (1.0 / 36.0,) * 12
relax_rate = 1.6
drag_factor = 20.0

FROM_X_HIGH = tuple(i for i in range(19) if lattice_speeds[i][0] == 1)
FROM_X_LOW = tuple(i for i in range(19) if lattice_speeds[i][0] == -1)
FROM_Y_HIGH = tuple(i for i in range(19) if lattice_speeds[i][1] == 1)
FROM_Y_LOW = tuple(i for i in range(19) if lattice_speeds[i][1] == -1)
CORNERS = tuple(i for i in range(19) if lattice_speeds[i][0] != 0 and lattice_speeds[i][1] != 0)


def opposite_of(number):
    return number + 1 if number % 2 == 1 else number - 1


def along_of(speed, flow):
    along = None
    for axis in range(3):
        if speed[axis] == 0:
            continue
        term = flow[axis] if speed[axis] == 1 else -flow[axis]
        along = term if along is None else along + term
    return along


def collide(moved, flow, fluid):
    speed_sq = flow[0] * flow[0] + flow[1] * flow[1] + flow[2] * flow[2]
    scalar_part = None
    vector_part = [None, None, None]
    drag_local = None
    for number in range(19):
        speed = lattice_speeds[number]
        weighted = lattice_weights[number] * moved[number]
        along = along_of(speed, flow)
        if along is None:
            scalar_term = weighted * (1.0 - 1.5 * speed_sq)
        else:
            scalar_term = weighted * (1.0 + 3.0 * along + 4.5 * along * along - 1.5 * speed_sq)
            drag_term = 3.0 * weighted * along
            drag_local = drag_term if drag_local is None else drag_local + drag_term
        scalar_part = scalar_term if scalar_part is None else scalar_part + scalar_term
        for axis in range(3):
            if speed[axis] == 0:
                term = weighted * (-3.0 * flow[axis])
            else:
                term = weighted * (3.0 * speed[axis] + 9.0 * along * speed[axis] - 3.0 * flow[axis])
            vector_part[axis] = term if vector_part[axis] is None else vector_part[axis] + term
    results = []
    for number in range(19):
        speed = lattice_speeds[number]
        projected = scalar_part
        for axis in range(3):
            projected = projected + vector_part[axis] * (speed[axis] - flow[axis])
        results.append(fluid * ((1.0 - relax_rate) * moved[number] + relax_rate * projected))
    return results, fluid * drag_local


def lbm_kernel(nx, ny, rows, lam_ref, vel_ref, blk_ref, fluid_ref, out_ref, drag_ref,
               moved, state, xhi, xlo, yhi, ylo, corner, part, row_buf, col_buf, row_sum,
               ssem, rsem, sum_send_a, sum_recv_a, sum_send_b, sum_recv_b):
    me_x = lax.axis_index("gx")
    me_y = lax.axis_index("gy")
    up_x = lax.rem(me_x + 1, nx)
    dn_x = lax.rem(me_x + nx - 1, nx)
    up_y = lax.rem(me_y + 1, ny)
    dn_y = lax.rem(me_y + ny - 1, ny)

    barrier = pltpu.get_barrier_semaphore()
    for k in range(1, ny):
        pl.semaphore_signal(barrier, inc=1, device_id=(me_x, lax.rem(me_y + k, ny)), device_id_type=MESH)
    for k in range(1, nx):
        pl.semaphore_signal(barrier, inc=1, device_id=(lax.rem(me_x + k, nx), me_y), device_id_type=MESH)
    for dev in ((up_x, up_y), (up_x, dn_y), (dn_x, up_y), (dn_x, dn_y)):
        pl.semaphore_signal(barrier, inc=1, device_id=dev, device_id_type=MESH)
    pl.semaphore_wait(barrier, nx + ny + 2)

    row8 = lax.broadcasted_iota(jnp.int32, (8, 128), 0)
    lane = lax.broadcasted_iota(jnp.int32, (rows, 128), 1)
    level = lax.rem(lax.broadcasted_iota(jnp.int32, (rows, 128), 0), 4)
    top = rows - 8
    drag_acc = jnp.zeros((8, 128), jnp.float32)

    for step in range(STEPS):
        src = lam_ref if step == 0 else state
        plan = []
        for j, number in enumerate(FROM_X_HIGH):
            plan.append((src.at[number, pl.ds(0, 8)], xhi.at[step, j], (dn_x, me_y)))
        for j, number in enumerate(FROM_X_LOW):
            plan.append((src.at[number, pl.ds(top, 8)], xlo.at[step, j], (up_x, me_y)))
        for j, number in enumerate(FROM_Y_HIGH):
            plan.append((src.at[number], yhi.at[step, j], (me_x, dn_y)))
        for j, number in enumerate(FROM_Y_LOW):
            plan.append((src.at[number], ylo.at[step, j], (me_x, up_y)))
        for j, number in enumerate(CORNERS):
            cx, cy, _ = lattice_speeds[number]
            rows_at = pl.ds(0, 8) if cx == 1 else pl.ds(top, 8)
            dev_x = dn_x if cx == 1 else up_x
            dev_y = dn_y if cy == 1 else up_y
            plan.append((src.at[number, rows_at], corner.at[step, j], (dev_x, dev_y)))
        copies = []
        for k, (from_ref, to_ref, dev) in enumerate(plan):
            copy = pltpu.make_async_remote_copy(
                src_ref=from_ref, dst_ref=to_ref, send_sem=ssem.at[step, k],
                recv_sem=rsem.at[step, k], device_id=dev, device_id_type=MESH)
            copy.start()
            copies.append(copy)
        for copy in copies:
            copy.wait()

        def patch_x(block, cx, tile):
            if cx == 1:
                head = jnp.where(row8 < 4, tile, block[0:8])
                return jnp.concatenate([head, block[8:]], axis=0)
            tail = jnp.where(row8 >= 4, tile, block[top:])
            return jnp.concatenate([block[:top], tail], axis=0)

        moved[0] = src[0]
        for number in range(1, 19):
            cx, cy, cz = lattice_speeds[number]
            own = src[number]
            if cx == 1:
                own = patch_x(own, cx, xhi[step, FROM_X_HIGH.index(number)])
            elif cx == -1:
                own = patch_x(own, cx, xlo[step, FROM_X_LOW.index(number)])
            if cy != 0:
                if cy == 1:
                    side = yhi[step, FROM_Y_HIGH.index(number)]
                else:
                    side = ylo[step, FROM_Y_LOW.index(number)]
                if cx != 0:
                    side = patch_x(side, cx, corner[step, CORNERS.index(number)])
                edge = 0 if cy == 1 else 127
                own = jnp.where(lane == edge, side, own)
            shift = 4 * cx + cz
            if shift % rows:
                own = pltpu.roll(own, (-shift) % rows, 0)
            if cy != 0:
                own = pltpu.roll(own, (-cy) % 128, 1)
            if cz == 1:
                own = jnp.where(level == 3, 0.0, own)
            elif cz == -1:
                own = jnp.where(level == 0, 0.0, own)
            bounced = src[opposite_of(number)] + 2.0 * cx
            moved[number] = jnp.where(blk_ref[number - 1] == 1, bounced, own)

        dest = out_ref if step == STEPS - 1 else state

        def chunk(c, acc):
            at = pl.ds(pl.multiple_of(c * 8, 8), 8)
            flow = [vel_ref[step, axis, at] for axis in range(3)]
            mu = [moved[number, at] for number in range(19)]
            fresh, drag = collide(mu, flow, fluid_ref[at])
            for number in range(19):
                dest[number, at] = fresh[number]
            return acc + drag

        drag_acc = lax.fori_loop(0, rows // 8, chunk, drag_acc)

    part[...] = jnp.broadcast_to(jnp.sum(drag_acc), (8, 128))

    row_copies = []
    for k in range(1, ny):
        copy = pltpu.make_async_remote_copy(
            src_ref=part, dst_ref=row_buf.at[me_y], send_sem=sum_send_a.at[k],
            recv_sem=sum_recv_a.at[k], device_id=(me_x, lax.rem(me_y + k, ny)),
            device_id_type=MESH)
        copy.start()
        row_copies.append(copy)
    row_buf[me_y] = part[...]
    for copy in row_copies:
        copy.wait()
    total = row_buf[0]
    for j in range(1, ny):
        total = total + row_buf[j]
    row_sum[...] = total

    col_copies = []
    for k in range(1, nx):
        copy = pltpu.make_async_remote_copy(
            src_ref=row_sum, dst_ref=col_buf.at[me_x], send_sem=sum_send_b.at[k],
            recv_sem=sum_recv_b.at[k], device_id=(lax.rem(me_x + k, nx), me_y),
            device_id_type=MESH)
        copy.start()
        col_copies.append(copy)
    col_buf[me_x] = total
    for copy in col_copies:
        copy.wait()
    total = col_buf[0]
    for j in range(1, nx):
        total = total + col_buf[j]
    drag_ref[...] = total


def per_device(adjoint_in, velocity, solid_tiles, link_blocked):
    nx = lax.axis_size("gx")
    ny = lax.axis_size("gy")
    q, rows_x, levels, rows_y = adjoint_in.shape
    rows = rows_x * levels
    lam = adjoint_in.reshape(q, rows, rows_y)
    flow = velocity.astype(jnp.float32).reshape(STEPS, 3, rows, rows_y)
    blocked = link_blocked.reshape(q - 1, rows, rows_y)
    solid = jnp.repeat(jnp.repeat(solid_tiles, TILE, axis=0), TILE, axis=2)
    fluid = (1.0 - solid.astype(jnp.float32)).reshape(rows, rows_y)
    n_copies = len(FROM_X_HIGH) + len(FROM_X_LOW) + len(FROM_Y_HIGH) + len(FROM_Y_LOW) + len(CORNERS)
    vmem = pl.BlockSpec(memory_space=pltpu.VMEM)
    state, drag = pl.pallas_call(
        functools.partial(lbm_kernel, nx, ny, rows),
        out_shape=(
            jax.ShapeDtypeStruct((q, rows, rows_y), jnp.float32),
            jax.ShapeDtypeStruct((8, 128), jnp.float32),
        ),
        in_specs=[vmem] * 4,
        out_specs=(vmem, vmem),
        scratch_shapes=[
            pltpu.VMEM((q, rows, rows_y), jnp.float32),
            pltpu.VMEM((q, rows, rows_y), jnp.float32),
            pltpu.VMEM((STEPS, len(FROM_X_HIGH), 8, rows_y), jnp.float32),
            pltpu.VMEM((STEPS, len(FROM_X_LOW), 8, rows_y), jnp.float32),
            pltpu.VMEM((STEPS, len(FROM_Y_HIGH), rows, rows_y), jnp.float32),
            pltpu.VMEM((STEPS, len(FROM_Y_LOW), rows, rows_y), jnp.float32),
            pltpu.VMEM((STEPS, len(CORNERS), 8, rows_y), jnp.float32),
            pltpu.VMEM((8, 128), jnp.float32),
            pltpu.VMEM((ny, 8, 128), jnp.float32),
            pltpu.VMEM((nx, 8, 128), jnp.float32),
            pltpu.VMEM((8, 128), jnp.float32),
            pltpu.SemaphoreType.DMA((STEPS, n_copies)),
            pltpu.SemaphoreType.DMA((STEPS, n_copies)),
            pltpu.SemaphoreType.DMA((ny,)),
            pltpu.SemaphoreType.DMA((ny,)),
            pltpu.SemaphoreType.DMA((nx,)),
            pltpu.SemaphoreType.DMA((nx,)),
        ],
        compiler_params=pltpu.CompilerParams(collective_id=0, has_side_effects=True),
    )(lam, flow, blocked, fluid)
    cell_count = rows_x * nx * rows_y * ny * levels
    scale = drag_factor / math.sqrt(cell_count)
    return (state.reshape(q, rows_x, levels, rows_y), (-scale * drag[0, 0]).reshape(1))


def solution(mesh):
    placed = (
        P(None, "gx", None, "gy"),
        P(None, None, "gx", None, "gy"),
        P("gx", None, "gy"),
        P(None, "gx", None, "gy"),
    )
    return jax.shard_map(
        per_device,
        mesh=mesh,
        in_specs=placed,
        out_specs=(P(None, "gx", None, "gy"), P()),
        check_vma=False,
    )
```

time: 153 us -> 71.6 us (0.47)
  starting transfers between devices: 45.7 us -> 0 us
  waiting for transfers between devices: 25.2 us -> 0 us
  Pallas kernels: 39 us -> 62.8 us
  local copies, waits for them, and re-layouts: 25.4 us -> 4.73 us
  other arithmetic: 12.2 us -> 1.39 us
  between operations: 4.66 us -> 2.43 us
    ppermute x8 -> x0, starting transfers between devices: 45.7 us -> none  [the longest x4 35 us: with_halo(): lax.ppermute(lax.slice_in_dim(block, 0, width, axis=dim), axis, backward)]
    ppermute x8 -> x0, waiting for transfers between devices: 25.2 us -> none  [the longest x4 25.2 us: with_halo(): lax.ppermute(lax.slice_in_dim(block, block.shape[dim] - width, None, axis...]
    pallas_call x1, Pallas kernels: 39 us -> 62.8 us  [per_device(): pl.pallas_call(functools.partial(lbm_kernel, nx, ny, rows), out_shape=(ja...]
    slice x32 -> x1, local copies, waits for them, and re-layouts: 14.5 us -> 1.18 us  [per_device(): drag[0, 0]]
    unnamed x36 -> x0, other arithmetic: 7.86 us -> none
    ppermute x4 -> x0, local copies, waits for them, and re-layouts: 4.97 us -> none  [the longest x2 2.89 us: with_halo(): lax.ppermute(lax.slice_in_dim(block, 0, width, axis=dim), axis, backward)]
    reduce_sum x2 -> x0, other arithmetic: 3.28 us -> none  [per_device(): step_terms.append(jnp.sum(drag_field))]
    unnamed x141 -> x3, local copies, waits for them, and re-layouts: 5 us -> 1.96 us
  transfers between devices with their start and end apart: 8 -> 0, of which waited for: 3 -> 0; matrix products, arithmetic and copies ran while one was open for 8% -> 0% of each run, Pallas kernels for 0% -> 0%
where the time goes in v2:
time: 71.6 us; the launch traced here: 71.4 us
  Pallas kernels  62.8 us (88%)
  local copies, waits for them, and re-layouts  4.73 us (7%)
  between operations  2.43 us (3%)
  other arithmetic  1.39 us (2%)
    pallas_call x1, Pallas kernels, per_device(): pl.pallas_call(functools.partial(lbm_kernel, nx, ny, rows), out_shape=(ja...  62.8 us
    unnamed x3, local copies, waits for them, and re-layouts  1.96 us

profile of v2, /device:TPU:1, one launch (start us, length us, event | category | flops | bytes accessed | tf_op | source)
XLA Modules:
  0.0 71.4 jit_solution(12196760272054482382)
XLA Ops:
  0.6 0.7 convert_subtract_fusion
  1.3 0.3 broadcast_in_dim.7
  1.7 0.0 copy-start
  1.7 1.2 %sub.18.fluid_ref = f32[64,128]{1,0:T(8,128)} reshape(f32[16,4,32,4]{3,2,1,0:T(8,128)S(1)} %broadcast_in_dim.7) | data formatting | bytes 65536 | tf_op jit(solution)/shard_map/sub | solution.py:238
  2.9 0.0 copy-done
  2.9 0.7 convert.1.vel_ref
  3.6 62.8 %shard_map.59 = (f32[19,64,128]{2,1,0:T(8,128)}, f32[8,128]{1,0:T(8,128)}) custom-call(f32[19,64,128]{2,1,0:T(8,128)} %bitcast.9, f32[2,3,64,128]{3,2,1,0:T(8,128)} %convert.1.vel_ref, s32[18,64,128]{2,1,0:T(8,128)} %bitcast.11, f32[64,128]{1,0:T(8,128)} %sub.18.fluid_ref), custom_call_target="tpu_custom_call" | custom-call | tf_op jit(solution)/shard_map/pallas_call | solution.py:241
  66.4 1.2 %slice.3 = f32[1,1]{1,0:T(1,128)} slice(f32[8,128]{1,0:T(8,128)} %get-tuple-element.5), slice={[0:1], [0:1]} | slice | bytes 8 | tf_op jit(solution)/shard_map/slice | solution.py:272
  68.3 2.0 %copy.7 = f32[19,16,4,128]{3,2,1,0:T(4,128)} copy(f32[19,16,4,128]{3,2,1,0:T(4,128)} %bitcast.10) | data formatting | bytes 1245184
  (1 shorter events, 0.0 us)
Async XLA Ops:
  1.7 1.3 %copy-start = (bf16[2,3,16,4,128]{4,3,2,1,0:T(4,128)(2,1)S(1)}, bf16[2,3,16,4,128]{4,3,2,1,0:T(4,128)(2,1)}, u32[]{:S(2)}) copy-start(bf16[2,3,16,4,128]{4,3,2,1,0:T(4,128)(2,1)} %param.5) | copy-start | bytes 294916

commit v3 on v2

v3 whole, which is shorter than its diff:
```python
import functools
import math

import jax
import jax.numpy as jnp
from jax import lax
from jax.experimental import pallas as pl
from jax.experimental.pallas import tpu as pltpu
from jax.sharding import PartitionSpec as P

MESH = pl.DeviceIdType.MESH
TILE = 4
STEPS = 2

lattice_speeds = (
    (0, 0, 0),
    (1, 0, 0),
    (-1, 0, 0),
    (0, 1, 0),
    (0, -1, 0),
    (0, 0, 1),
    (0, 0, -1),
    (1, 1, 0),
    (-1, -1, 0),
    (1, -1, 0),
    (-1, 1, 0),
    (1, 0, 1),
    (-1, 0, -1),
    (1, 0, -1),
    (-1, 0, 1),
    (0, 1, 1),
    (0, -1, -1),
    (0, 1, -1),
    (0, -1, 1),
)
lattice_weights = (1.0 / 3.0,) + (1.0 / 18.0,) * 6 + (1.0 / 36.0,) * 12
relax_rate = 1.6
drag_factor = 20.0


def crossing(speeds):
    return (
        tuple(n for n, c in speeds if c[0] == 1),
        tuple(n for n, c in speeds if c[0] == -1),
        tuple(n for n, c in speeds if c[1] == 1),
        tuple(n for n, c in speeds if c[1] == -1),
        tuple(n for n, c in speeds if c[0] != 0 and c[1] != 0),
    )


MOVING = tuple((n, lattice_speeds[n]) for n in range(1, 19))
REVERSED = tuple((n, tuple(-v for v in lattice_speeds[n])) for n in range(1, 19))
N_COPIES = sum(len(s) for s in crossing(MOVING))


def opposite_of(number):
    return number + 1 if number % 2 == 1 else number - 1


def along_of(speed, flow):
    along = None
    for axis in range(3):
        if speed[axis] == 0:
            continue
        term = flow[axis] if speed[axis] == 1 else -flow[axis]
        along = term if along is None else along + term
    return along


def collide(moved, flow, fluid):
    speed_sq = flow[0] * flow[0] + flow[1] * flow[1] + flow[2] * flow[2]
    scalar_part = None
    vector_part = [None, None, None]
    drag_local = None
    for number in range(19):
        speed = lattice_speeds[number]
        weighted = lattice_weights[number] * moved[number]
        along = along_of(speed, flow)
        if along is None:
            scalar_term = weighted * (1.0 - 1.5 * speed_sq)
        else:
            scalar_term = weighted * (1.0 + 3.0 * along + 4.5 * along * along - 1.5 * speed_sq)
            drag_term = 3.0 * weighted * along
            drag_local = drag_term if drag_local is None else drag_local + drag_term
        scalar_part = scalar_term if scalar_part is None else scalar_part + scalar_term
        for axis in range(3):
            if speed[axis] == 0:
                term = weighted * (-3.0 * flow[axis])
            else:
                term = weighted * (3.0 * speed[axis] + 9.0 * along * speed[axis] - 3.0 * flow[axis])
            vector_part[axis] = term if vector_part[axis] is None else vector_part[axis] + term
    results = []
    for number in range(19):
        speed = lattice_speeds[number]
        projected = scalar_part
        for axis in range(3):
            projected = projected + vector_part[axis] * (speed[axis] - flow[axis])
        results.append(fluid * ((1.0 - relax_rate) * moved[number] + relax_rate * projected))
    return results, fluid * drag_local


def send_plan(sets, speeds, field, bufs, top, near):
    up_x, dn_x, up_y, dn_y, me_x, me_y = near
    x_high, x_low, y_high, y_low, corners = sets
    xhi, xlo, yhi, ylo, corner = bufs
    plan = []
    for j, n in enumerate(x_high):
        plan.append((field(n).at[pl.ds(0, 8)], xhi.at[j], (dn_x, me_y)))
    for j, n in enumerate(x_low):
        plan.append((field(n).at[pl.ds(top, 8)], xlo.at[j], (up_x, me_y)))
    for j, n in enumerate(y_high):
        plan.append((field(n), yhi.at[j], (me_x, dn_y)))
    for j, n in enumerate(y_low):
        plan.append((field(n), ylo.at[j], (me_x, up_y)))
    for j, n in enumerate(corners):
        cx, cy, _ = speeds[n]
        rows_at = pl.ds(0, 8) if cx == 1 else pl.ds(top, 8)
        dev_x = dn_x if cx == 1 else up_x
        dev_y = dn_y if cy == 1 else up_y
        plan.append((field(n).at[rows_at], corner.at[j], (dev_x, dev_y)))
    return plan


def start_copies(plan, send_sems, recv_sems):
    copies = []
    for k, (from_ref, to_ref, dev) in enumerate(plan):
        copy = pltpu.make_async_remote_copy(
            src_ref=from_ref, dst_ref=to_ref, send_sem=send_sems.at[k],
            recv_sem=recv_sems.at[k], device_id=dev, device_id_type=MESH)
        copy.start()
        copies.append(copy)
    return copies


def shifted(own, speed, n, sets, bufs, rows):
    x_high, x_low, y_high, y_low, corners = sets
    xhi, xlo, yhi, ylo, corner = bufs
    cx, cy, cz = speed
    top = rows - 8
    row8 = lax.broadcasted_iota(jnp.int32, (8, 128), 0)
    lane = lax.broadcasted_iota(jnp.int32, (rows, 128), 1)
    level = lax.rem(lax.broadcasted_iota(jnp.int32, (rows, 128), 0), 4)

    def patch_x(block, tile):
        if cx == 1:
            head = jnp.where(row8 < 4, tile, block[0:8])
            return jnp.concatenate([head, block[8:]], axis=0)
        tail = jnp.where(row8 >= 4, tile, block[top:])
        return jnp.concatenate([block[:top], tail], axis=0)

    if cx == 1:
        own = patch_x(own, xhi[x_high.index(n)])
    elif cx == -1:
        own = patch_x(own, xlo[x_low.index(n)])
    if cy != 0:
        side = yhi[y_high.index(n)] if cy == 1 else ylo[y_low.index(n)]
        if cx != 0:
            side = patch_x(side, corner[corners.index(n)])
        edge = 0 if cy == 1 else 127
        own = jnp.where(lane == edge, side, own)
    shift = 4 * cx + cz
    if shift % rows:
        own = pltpu.roll(own, (-shift) % rows, 0)
    if cy != 0:
        own = pltpu.roll(own, (-cy) % 128, 1)
    if cz == 1:
        own = jnp.where(level == 3, 0.0, own)
    elif cz == -1:
        own = jnp.where(level == 0, 0.0, own)
    return own


def drag_weight(number, flow, fluid):
    return (3.0 * lattice_weights[number]) * along_of(lattice_speeds[number], flow) * fluid


def lbm_kernel(nx, ny, rows, lam_ref, vel_ref, blk_ref, fluid_ref, out_ref, drag_ref,
               moved, state, hfield, xhi, xlo, yhi, ylo, corner, hxhi, hxlo, hyhi, hylo, hcorner,
               part, row_buf, col_buf, row_sum,
               ssem, rsem, hsend, hrecv, sum_send_a, sum_recv_a, sum_send_b, sum_recv_b):
    me_x = lax.axis_index("gx")
    me_y = lax.axis_index("gy")
    up_x = lax.rem(me_x + 1, nx)
    dn_x = lax.rem(me_x + nx - 1, nx)
    up_y = lax.rem(me_y + 1, ny)
    dn_y = lax.rem(me_y + ny - 1, ny)
    near = (up_x, dn_x, up_y, dn_y, me_x, me_y)
    top = rows - 8

    barrier = pltpu.get_barrier_semaphore()
    for k in range(1, ny):
        pl.semaphore_signal(barrier, inc=1, device_id=(me_x, lax.rem(me_y + k, ny)), device_id_type=MESH)
    for k in range(1, nx):
        pl.semaphore_signal(barrier, inc=1, device_id=(lax.rem(me_x + k, nx), me_y), device_id_type=MESH)
    for dev in ((up_x, up_y), (up_x, dn_y), (dn_x, up_y), (dn_x, dn_y)):
        pl.semaphore_signal(barrier, inc=1, device_id=dev, device_id_type=MESH)

    last_flow = [vel_ref[STEPS - 1, axis] for axis in range(3)]
    fluid_all = fluid_ref[...]
    for number in range(1, 19):
        weight = drag_weight(number, last_flow, fluid_all)
        hfield[number - 1] = jnp.where(blk_ref[number - 1] == 1, 0.0, weight)

    pl.semaphore_wait(barrier, nx + ny + 2)

    lam_sets = crossing(MOVING)
    h_sets = crossing(REVERSED)
    h_speeds = dict(REVERSED)
    lam_speeds = dict(MOVING)
    h_bufs = (hxhi, hxlo, hyhi, hylo, hcorner)
    h_copies = None
    drag_acc = jnp.zeros((8, 128), jnp.float32)

    for step in range(STEPS):
        src = lam_ref if step == 0 else state
        bufs = (xhi.at[step], xlo.at[step], yhi.at[step], ylo.at[step], corner.at[step])
        plan = send_plan(lam_sets, lam_speeds, lambda n: src.at[n], bufs, top, near)
        copies = start_copies(plan, ssem.at[step], rsem.at[step])
        if step == 0:
            h_plan = send_plan(h_sets, h_speeds, lambda n: hfield.at[n - 1], h_bufs, top, near)
            h_copies = start_copies(h_plan, hsend, hrecv)
        if step == STEPS - 1:
            for copy in h_copies:
                copy.wait()
            total = drag_acc
            for number in range(1, 19):
                gathered = shifted(hfield[number - 1], h_speeds[number], number, h_sets, h_bufs, rows)
                total = total + jnp.sum((src[number] * gathered).reshape(rows // 8, 8, 128), axis=0)
            for number in range(1, 19):
                cx = lattice_speeds[number][0]
                weight = drag_weight(number, last_flow, fluid_all)
                bounced = jnp.where(blk_ref[number - 1] == 1, src[opposite_of(number)] + 2.0 * cx, 0.0)
                total = total + jnp.sum((weight * bounced).reshape(rows // 8, 8, 128), axis=0)
            part[...] = jnp.broadcast_to(jnp.sum(total), (8, 128))
            row_copies = []
            for k in range(1, ny):
                copy = pltpu.make_async_remote_copy(
                    src_ref=part, dst_ref=row_buf.at[me_y], send_sem=sum_send_a.at[k],
                    recv_sem=sum_recv_a.at[k], device_id=(me_x, lax.rem(me_y + k, ny)),
                    device_id_type=MESH)
                copy.start()
                row_copies.append(copy)
            row_buf[me_y] = part[...]
        for copy in copies:
            copy.wait()

        moved[0] = src[0]
        for number in range(1, 19):
            source = shifted(src[number], lam_speeds[number], number, lam_sets, bufs, rows)
            bounced = src[opposite_of(number)] + 2.0 * lam_speeds[number][0]
            moved[number] = jnp.where(blk_ref[number - 1] == 1, bounced, source)

        if step == STEPS - 1:
            for copy in row_copies:
                copy.wait()
            total = row_buf[0]
            for j in range(1, ny):
                total = total + row_buf[j]
            row_sum[...] = total
            col_copies = []
            for k in range(1, nx):
                copy = pltpu.make_async_remote_copy(
                    src_ref=row_sum, dst_ref=col_buf.at[me_x], send_sem=sum_send_b.at[k],
                    recv_sem=sum_recv_b.at[k], device_id=(lax.rem(me_x + k, nx), me_y),
                    device_id_type=MESH)
                copy.start()
                col_copies.append(copy)
            col_buf[me_x] = total

        dest = out_ref if step == STEPS - 1 else state

        def chunk(c, acc):
            at = pl.ds(pl.multiple_of(c * 8, 8), 8)
            flow = [vel_ref[step, axis, at] for axis in range(3)]
            mu = [moved[number, at] for number in range(19)]
            fresh, drag = collide(mu, flow, fluid_ref[at])
            for number in range(19):
                dest[number, at] = fresh[number]
            return acc + drag

        if step < STEPS - 1:
            drag_acc = lax.fori_loop(0, rows // 8, chunk, drag_acc)
        else:
            lax.fori_loop(0, rows // 8, chunk, drag_acc)

    for copy in col_copies:
        copy.wait()
    total = col_buf[0]
    for j in range(1, nx):
        total = total + col_buf[j]
    drag_ref[...] = total


def per_device(adjoint_in, velocity, solid_tiles, link_blocked):
    nx = lax.axis_size("gx")
    ny = lax.axis_size("gy")
    q, rows_x, levels, rows_y = adjoint_in.shape
    rows = rows_x * levels
    lam = adjoint_in.reshape(q, rows, rows_y)
    flow = velocity.astype(jnp.float32).reshape(STEPS, 3, rows, rows_y)
    blocked = link_blocked.reshape(q - 1, rows, rows_y)
    solid = jnp.repeat(jnp.repeat(solid_tiles, TILE, axis=0), TILE, axis=2)
    fluid = (1.0 - solid.astype(jnp.float32)).reshape(rows, rows_y)
    vmem = pl.BlockSpec(memory_space=pltpu.VMEM)
    state, drag = pl.pallas_call(
        functools.partial(lbm_kernel, nx, ny, rows),
        out_shape=(
            jax.ShapeDtypeStruct((q, rows, rows_y), jnp.float32),
            jax.ShapeDtypeStruct((8, 128), jnp.float32),
        ),
        in_specs=[vmem] * 4,
        out_specs=(vmem, vmem),
        scratch_shapes=[
            pltpu.VMEM((q, rows, rows_y), jnp.float32),
            pltpu.VMEM((q, rows, rows_y), jnp.float32),
            pltpu.VMEM((q - 1, rows, rows_y), jnp.float32),
        ]
        + [
            pltpu.VMEM((STEPS, len(s), rows if face >= 2 and face < 4 else 8, rows_y), jnp.float32)
            for face, s in enumerate(crossing(MOVING))
        ]
        + [
            pltpu.VMEM((len(s), rows if face >= 2 and face < 4 else 8, rows_y), jnp.float32)
            for face, s in enumerate(crossing(REVERSED))
        ]
        + [
            pltpu.VMEM((8, 128), jnp.float32),
            pltpu.VMEM((ny, 8, 128), jnp.float32),
            pltpu.VMEM((nx, 8, 128), jnp.float32),
            pltpu.VMEM((8, 128), jnp.float32),
            pltpu.SemaphoreType.DMA((STEPS, N_COPIES)),
            pltpu.SemaphoreType.DMA((STEPS, N_COPIES)),
            pltpu.SemaphoreType.DMA((N_COPIES,)),
            pltpu.SemaphoreType.DMA((N_COPIES,)),
            pltpu.SemaphoreType.DMA((ny,)),
            pltpu.SemaphoreType.DMA((ny,)),
            pltpu.SemaphoreType.DMA((nx,)),
            pltpu.SemaphoreType.DMA((nx,)),
        ],
        compiler_params=pltpu.CompilerParams(collective_id=0, has_side_effects=True),
    )(lam, flow, blocked, fluid)
    cell_count = rows_x * nx * rows_y * ny * levels
    scale = drag_factor / math.sqrt(cell_count)
    return (state.reshape(q, rows_x, levels, rows_y), (-scale * drag[0, 0]).reshape(1))


def solution(mesh):
    placed = (
        P(None, "gx", None, "gy"),
        P(None, None, "gx", None, "gy"),
        P("gx", None, "gy"),
        P(None, "gx", None, "gy"),
    )
    return jax.shard_map(
        per_device,
        mesh=mesh,
        in_specs=placed,
        out_specs=(P(None, "gx", None, "gy"), P()),
        check_vma=False,
    )
```

time: 71.6 us -> 64.5 us (0.901)
  Pallas kernels: 62.8 us -> 55.7 us
    pallas_call x1, Pallas kernels: 62.8 us -> 55.7 us  [per_device(): pl.pallas_call(functools.partial(lbm_kernel, nx, ny, rows), out_shape=(ja...]
where the time goes in v3:
time: 64.5 us; the launch traced here: 64.2 us
  Pallas kernels  55.7 us (86%)
  local copies, waits for them, and re-layouts  4.73 us (7%)
  between operations  2.43 us (4%)
  other arithmetic  1.39 us (2%)
    pallas_call x1, Pallas kernels, per_device(): pl.pallas_call(functools.partial(lbm_kernel, nx, ny, rows), out_shape=(ja...  55.7 us
    unnamed x3, local copies, waits for them, and re-layouts  1.96 us

profile of v3, /device:TPU:1, one launch (start us, length us, event | category | flops | bytes accessed | tf_op | source)
XLA Modules:
  0.0 64.2 jit_solution(8650130084101341378)
XLA Ops:
  0.6 0.7 %convert_subtract_fusion = f32[4,4,32]{2,1,0:T(4,128)S(1)} fusion(s32[4,4,32]{2,1,0:T(4,128)} %param.6), kind=kLoop, calls=%fused_computation | loop fusion | flops 1024 | bytes 4096 | tf_op jit(solution)/shard_map/sub | solution.py:303
  1.3 0.3 broadcast_in_dim.7
  1.7 0.0 copy-start
  1.7 1.2 %sub.18.fluid_ref = f32[64,128]{1,0:T(8,128)} reshape(f32[16,4,32,4]{3,2,1,0:T(8,128)S(1)} %broadcast_in_dim.7) | data formatting | bytes 65536 | tf_op jit(solution)/shard_map/sub | solution.py:303
  2.9 0.0 copy-done
  2.9 0.7 %convert.1.vel_ref = f32[2,3,64,128]{3,2,1,0:T(8,128)} convert(bf16[2,3,64,128]{3,2,1,0:T(8,128)(2,1)S(1)} %bitcast.13) | non-fusion elementwise | flops 49152 | bytes 294912 | tf_op jit(solution)/shard_map/reshape | solution.py:300
  3.6 55.7 %shard_map.59 = (f32[19,64,128]{2,1,0:T(8,128)}, f32[8,128]{1,0:T(8,128)}) custom-call(f32[19,64,128]{2,1,0:T(8,128)} %bitcast.9, f32[2,3,64,128]{3,2,1,0:T(8,128)} %convert.1.vel_ref, s32[18,64,128]{2,1,0:T(8,128)} %bitcast.11, f32[64,128]{1,0:T(8,128)} %sub.18.fluid_ref), custom_call_target="tpu_custom_call" | custom-call | tf_op jit(solution)/shard_map/pallas_call | solution.py:305
  59.3 1.2 %slice.3 = f32[1,1]{1,0:T(1,128)} slice(f32[8,128]{1,0:T(8,128)} %get-tuple-element.5), slice={[0:1], [0:1]} | slice | bytes 8 | tf_op jit(solution)/shard_map/slice | solution.py:344
  61.2 2.0 %copy.7 = f32[19,16,4,128]{3,2,1,0:T(4,128)} copy(f32[19,16,4,128]{3,2,1,0:T(4,128)} %bitcast.10) | data formatting | bytes 1245184
  (1 shorter events, 0.0 us)
Async XLA Ops:
  1.7 1.3 %copy-start = (bf16[2,3,16,4,128]{4,3,2,1,0:T(4,128)(2,1)S(1)}, bf16[2,3,16,4,128]{4,3,2,1,0:T(4,128)(2,1)}, u32[]{:S(2)}) copy-start(bf16[2,3,16,4,128]{4,3,2,1,0:T(4,128)(2,1)} %param.5) | copy-start | bytes 294916

commit v4 on v3

--- a/solution.py
+++ b/solution.py
@@ -174,8 +174,8 @@
     return (3.0 * lattice_weights[number]) * along_of(lattice_speeds[number], flow) * fluid
 
 
-def lbm_kernel(nx, ny, rows, lam_ref, vel_ref, blk_ref, fluid_ref, out_ref, drag_ref,
-               moved, state, hfield, xhi, xlo, yhi, ylo, corner, hxhi, hxlo, hyhi, hylo, hcorner,
+def lbm_kernel(nx, ny, rows, scale, lam_ref, vel_in, blk_ref, out_ref, drag_ref,
+               vel_ref, fluid_ref, moved, state, hfield, xhi, xlo, yhi, ylo, corner, hxhi, hxlo, hyhi, hylo, hcorner,
                part, row_buf, col_buf, row_sum,
                ssem, rsem, hsend, hrecv, sum_send_a, sum_recv_a, sum_send_b, sum_recv_b):
     me_x = lax.axis_index("gx")
@@ -194,6 +194,15 @@
         pl.semaphore_signal(barrier, inc=1, device_id=(lax.rem(me_x + k, nx), me_y), device_id_type=MESH)
     for dev in ((up_x, up_y), (up_x, dn_y), (dn_x, up_y), (dn_x, dn_y)):
         pl.semaphore_signal(barrier, inc=1, device_id=dev, device_id_type=MESH)
+
+    for step in range(STEPS):
+        for axis in range(3):
+            vel_ref[step, axis] = vel_in[step, axis].astype(jnp.float32)
+    level = lax.rem(lax.broadcasted_iota(jnp.int32, (rows, 128), 0), 4)
+    from_below = pltpu.roll(blk_ref[4], 1, 0)
+    from_above = pltpu.roll(blk_ref[5], rows - 1, 0)
+    solid = jnp.where(level == 3, from_below, from_above)
+    fluid_ref[...] = 1.0 - solid.astype(jnp.float32)
 
     last_flow = [vel_ref[STEPS - 1, axis] for axis in range(3)]
     fluid_all = fluid_ref[...]
@@ -288,7 +297,7 @@
     total = col_buf[0]
     for j in range(1, nx):
         total = total + col_buf[j]
-    drag_ref[...] = total
+    drag_ref[0] = -scale * total[0, 0]
 
 
 def per_device(adjoint_in, velocity, solid_tiles, link_blocked):
@@ -297,20 +306,22 @@
     q, rows_x, levels, rows_y = adjoint_in.shape
     rows = rows_x * levels
     lam = adjoint_in.reshape(q, rows, rows_y)
-    flow = velocity.astype(jnp.float32).reshape(STEPS, 3, rows, rows_y)
+    flow = velocity.reshape(STEPS, 3, rows, rows_y)
     blocked = link_blocked.reshape(q - 1, rows, rows_y)
-    solid = jnp.repeat(jnp.repeat(solid_tiles, TILE, axis=0), TILE, axis=2)
-    fluid = (1.0 - solid.astype(jnp.float32)).reshape(rows, rows_y)
+    cell_count = rows_x * nx * rows_y * ny * levels
+    scale = drag_factor / math.sqrt(cell_count)
     vmem = pl.BlockSpec(memory_space=pltpu.VMEM)
     state, drag = pl.pallas_call(
-        functools.partial(lbm_kernel, nx, ny, rows),
+        functools.partial(lbm_kernel, nx, ny, rows, scale),
         out_shape=(
             jax.ShapeDtypeStruct((q, rows, rows_y), jnp.float32),
-            jax.ShapeDtypeStruct((8, 128), jnp.float32),
+            jax.ShapeDtypeStruct((1,), jnp.float32),
         ),
-        in_specs=[vmem] * 4,
-        out_specs=(vmem, vmem),
+        in_specs=[vmem] * 3,
+        out_specs=(vmem, pl.BlockSpec(memory_space=pltpu.SMEM)),
         scratch_shapes=[
+            pltpu.VMEM((STEPS, 3, rows, rows_y), jnp.float32),
+            pltpu.VMEM((rows, rows_y), jnp.float32),
             pltpu.VMEM((q, rows, rows_y), jnp.float32),
             pltpu.VMEM((q, rows, rows_y), jnp.float32),
             pltpu.VMEM((q - 1, rows, rows_y), jnp.float32),
@@ -338,10 +349,8 @@
             pltpu.SemaphoreType.DMA((nx,)),
         ],
         compiler_params=pltpu.CompilerParams(collective_id=0, has_side_effects=True),
-    )(lam, flow, blocked, fluid)
-    cell_count = rows_x * nx * rows_y * ny * levels
-    scale = drag_factor / math.sqrt(cell_count)
-    return (state.reshape(q, rows_x, levels, rows_y), (-scale * drag[0, 0]).reshape(1))
+    )(lam, flow, blocked)
+    return (state.reshape(q, rows_x, levels, rows_y), drag)
 
 
 def solution(mesh):

time: 64.5 us -> 60.2 us (0.933)
  local copies, waits for them, and re-layouts: 4.73 us -> 1.96 us
  other arithmetic: 1.39 us -> 0 us
    sub x1 -> x0, local copies, waits for them, and re-layouts: 1.24 us -> none  [per_device(): fluid = (1.0 - solid.astype(jnp.float32)).reshape(rows, rows_y)]
    slice x1 -> x0, local copies, waits for them, and re-layouts: 1.18 us -> none  [per_device(): drag[0, 0]]
    sub x1 -> x0, other arithmetic: 0.7 us -> none  [per_device(): fluid = (1.0 - solid.astype(jnp.float32)).reshape(rows, rows_y)]
    reshape x1 -> x0, other arithmetic: 0.69 us -> none  [per_device(): flow = velocity.astype(jnp.float32).reshape(STEPS, 3, rows, rows_y)]
    unnamed x3 -> x1, local copies, waits for them, and re-layouts: 1.96 us -> 1.96 us
where the time goes in v4:
time: 60.2 us; the launch traced here: 59.9 us
  Pallas kernels  55.7 us (93%)
  between operations  2.33 us (4%)
  local copies, waits for them, and re-layouts  1.96 us (3%)
    pallas_call x1, Pallas kernels, per_device(): pl.pallas_call(functools.partial(lbm_kernel, nx, ny, rows, scale), out_sh...  55.7 us
    unnamed x1, local copies, waits for them, and re-layouts  1.96 us

profile of v4, /device:TPU:1, one launch (start us, length us, event | category | flops | bytes accessed | tf_op | source)
XLA Modules:
  0.0 59.9 jit_solution(15499073091823456145)
XLA Ops:
  0.6 55.7 %shard_map.50 = (f32[19,64,128]{2,1,0:T(8,128)}, f32[1]{0:T(128)}) custom-call(f32[19,64,128]{2,1,0:T(8,128)} %bitcast.4, bf16[2,3,64,128]{3,2,1,0:T(8,128)(2,1)} %bitcast.7, s32[18,64,128]{2,1,0:T(8,128)} %bitcast.6), custom_call_target="tpu_custom_call" | custom-call | tf_op jit(solution)/shard_map/pallas_call | solution.py:314
  56.3 2.0 %copy.7 = f32[19,16,4,128]{3,2,1,0:T(4,128)} copy(f32[19,16,4,128]{3,2,1,0:T(4,128)} %bitcast.5) | data formatting | bytes 1245184

commit v5 on v4

--- a/solution.py
+++ b/solution.py
@@ -218,6 +218,7 @@
     lam_speeds = dict(MOVING)
     h_bufs = (hxhi, hxlo, hyhi, hylo, hcorner)
     h_copies = None
+    sent = []
     drag_acc = jnp.zeros((8, 128), jnp.float32)
 
     for step in range(STEPS):
@@ -230,7 +231,8 @@
             h_copies = start_copies(h_plan, hsend, hrecv)
         if step == STEPS - 1:
             for copy in h_copies:
-                copy.wait()
+                copy.wait_recv()
+            sent += h_copies
             total = drag_acc
             for number in range(1, 19):
                 gathered = shifted(hfield[number - 1], h_speeds[number], number, h_sets, h_bufs, rows)
@@ -251,7 +253,8 @@
                 row_copies.append(copy)
             row_buf[me_y] = part[...]
         for copy in copies:
-            copy.wait()
+            copy.wait_recv()
+        sent += copies
 
         moved[0] = src[0]
         for number in range(1, 19):
@@ -261,7 +264,8 @@
 
         if step == STEPS - 1:
             for copy in row_copies:
-                copy.wait()
+                copy.wait_recv()
+            sent += row_copies
             total = row_buf[0]
             for j in range(1, ny):
                 total = total + row_buf[j]
@@ -293,11 +297,14 @@
             lax.fori_loop(0, rows // 8, chunk, drag_acc)
 
     for copy in col_copies:
-        copy.wait()
+        copy.wait_recv()
+    sent += col_copies
     total = col_buf[0]
     for j in range(1, nx):
         total = total + col_buf[j]
     drag_ref[0] = -scale * total[0, 0]
+    for copy in sent:
+        copy.wait_send()
 
 
 def per_device(adjoint_in, velocity, solid_tiles, link_blocked):

time: 60.2 us -> 60.3 us (level)
  no operation moved by 1% of the time
where the time goes in v5:
time: 60.3 us; the launch traced here: 60.1 us
  Pallas kernels  55.8 us (93%)
  between operations  2.33 us (4%)
  local copies, waits for them, and re-layouts  1.96 us (3%)
    pallas_call x1, Pallas kernels, per_device(): pl.pallas_call(functools.partial(lbm_kernel, nx, ny, rows, scale), out_sh...  55.8 us
    unnamed x1, local copies, waits for them, and re-layouts  1.96 us

profile of v5, /device:TPU:1, one launch (start us, length us, event | category | flops | bytes accessed | tf_op | source)
XLA Modules:
  0.0 60.1 jit_solution(17819414455825484802)
XLA Ops:
  0.6 55.8 %shard_map.50 = (f32[19,64,128]{2,1,0:T(8,128)}, f32[1]{0:T(128)}) custom-call(f32[19,64,128]{2,1,0:T(8,128)} %bitcast.4, bf16[2,3,64,128]{3,2,1,0:T(8,128)(2,1)} %bitcast.7, s32[18,64,128]{2,1,0:T(8,128)} %bitcast.6), custom_call_target="tpu_custom_call" | custom-call | tf_op jit(solution)/shard_map/pallas_call | solution.py:321
  56.5 2.0 %copy.7 = f32[19,16,4,128]{3,2,1,0:T(4,128)} copy(f32[19,16,4,128]{3,2,1,0:T(4,128)} %bitcast.5) | data formatting | bytes 1245184

commit v6 on v5

--- a/solution.py
+++ b/solution.py
@@ -174,8 +174,8 @@
     return (3.0 * lattice_weights[number]) * along_of(lattice_speeds[number], flow) * fluid
 
 
-def lbm_kernel(nx, ny, rows, scale, lam_ref, vel_in, blk_ref, out_ref, drag_ref,
-               vel_ref, fluid_ref, moved, state, hfield, xhi, xlo, yhi, ylo, corner, hxhi, hxlo, hyhi, hylo, hcorner,
+def lbm_kernel(nx, ny, rows, scale, lam_hbm, vel_hbm, blk_hbm, out_ref, drag_ref,
+               lam_ref, vel_in, blk_ref, load_sem, vel_ref, fluid_ref, moved, state, hfield, xhi, xlo, yhi, ylo, corner, hxhi, hxlo, hyhi, hylo, hcorner,
                part, row_buf, col_buf, row_sum,
                ssem, rsem, hsend, hrecv, sum_send_a, sum_recv_a, sum_send_b, sum_recv_b):
     me_x = lax.axis_index("gx")
@@ -187,6 +187,13 @@
     near = (up_x, dn_x, up_y, dn_y, me_x, me_y)
     top = rows - 8
 
+    loads = [
+        pltpu.make_async_copy(hbm, vmem, load_sem.at[k])
+        for k, (hbm, vmem) in enumerate(((lam_hbm, lam_ref), (vel_hbm, vel_in), (blk_hbm, blk_ref)))
+    ]
+    for load in loads:
+        load.start()
+
     barrier = pltpu.get_barrier_semaphore()
     for k in range(1, ny):
         pl.semaphore_signal(barrier, inc=1, device_id=(me_x, lax.rem(me_y + k, ny)), device_id_type=MESH)
@@ -195,6 +202,8 @@
     for dev in ((up_x, up_y), (up_x, dn_y), (dn_x, up_y), (dn_x, dn_y)):
         pl.semaphore_signal(barrier, inc=1, device_id=dev, device_id_type=MESH)
 
+    loads[1].wait()
+    loads[2].wait()
     for step in range(STEPS):
         for axis in range(3):
             vel_ref[step, axis] = vel_in[step, axis].astype(jnp.float32)
@@ -223,8 +232,9 @@
 
     for step in range(STEPS):
         src = lam_ref if step == 0 else state
+        origin = lam_hbm if step == 0 else state
         bufs = (xhi.at[step], xlo.at[step], yhi.at[step], ylo.at[step], corner.at[step])
-        plan = send_plan(lam_sets, lam_speeds, lambda n: src.at[n], bufs, top, near)
+        plan = send_plan(lam_sets, lam_speeds, lambda n: origin.at[n], bufs, top, near)
         copies = start_copies(plan, ssem.at[step], rsem.at[step])
         if step == 0:
             h_plan = send_plan(h_sets, h_speeds, lambda n: hfield.at[n - 1], h_bufs, top, near)
@@ -252,6 +262,8 @@
                 copy.start()
                 row_copies.append(copy)
             row_buf[me_y] = part[...]
+        if step == 0:
+            loads[0].wait()
         for copy in copies:
             copy.wait_recv()
         sent += copies
@@ -324,9 +336,13 @@
             jax.ShapeDtypeStruct((q, rows, rows_y), jnp.float32),
             jax.ShapeDtypeStruct((1,), jnp.float32),
         ),
-        in_specs=[vmem] * 3,
+        in_specs=[pl.BlockSpec(memory_space=pl.ANY)] * 3,
         out_specs=(vmem, pl.BlockSpec(memory_space=pltpu.SMEM)),
         scratch_shapes=[
+            pltpu.VMEM((q, rows, rows_y), jnp.float32),
+            pltpu.VMEM((STEPS, 3, rows, rows_y), velocity.dtype),
+            pltpu.VMEM((q - 1, rows, rows_y), link_blocked.dtype),
+            pltpu.SemaphoreType.DMA((3,)),
             pltpu.VMEM((STEPS, 3, rows, rows_y), jnp.float32),
             pltpu.VMEM((rows, rows_y), jnp.float32),
             pltpu.VMEM((q, rows, rows_y), jnp.float32),

time: 60.3 us -> 59.1 us (0.980)
  Pallas kernels: 55.8 us -> 54.6 us
    pallas_call x1, Pallas kernels: 55.8 us -> 54.6 us  [per_device(): pl.pallas_call(functools.partial(lbm_kernel, nx, ny, rows, scale), out_sh...]
where the time goes in v6:
time: 59.1 us; the launch traced here: 58.9 us
  Pallas kernels  54.6 us (92%)
  between operations  2.33 us (4%)
  local copies, waits for them, and re-layouts  1.96 us (3%)
    pallas_call x1, Pallas kernels, per_device(): pl.pallas_call(functools.partial(lbm_kernel, nx, ny, rows, scale), out_sh...  54.6 us
    unnamed x1, local copies, waits for them, and re-layouts  1.96 us

profile of v6, /device:TPU:1, one launch (start us, length us, event | category | flops | bytes accessed | tf_op | source)
XLA Modules:
  0.0 58.9 jit_solution(5221360336772433998)
XLA Ops:
  0.6 54.6 %shard_map.50 = (f32[19,64,128]{2,1,0:T(8,128)}, f32[1]{0:T(128)}) custom-call(f32[19,64,128]{2,1,0:T(8,128)} %bitcast.4, bf16[2,3,64,128]{3,2,1,0:T(8,128)(2,1)} %bitcast.7, s32[18,64,128]{2,1,0:T(8,128)} %bitcast.6), custom_call_target="tpu_custom_call" | custom-call | tf_op jit(solution)/shard_map/pallas_call | solution.py:333
  55.2 2.0 %copy.7 = f32[19,16,4,128]{3,2,1,0:T(4,128)} copy(f32[19,16,4,128]{3,2,1,0:T(4,128)} %bitcast.5) | data formatting | bytes 1245184

commit v7 on v6

--- a/solution.py
+++ b/solution.py
@@ -50,7 +50,7 @@
 
 MOVING = tuple((n, lattice_speeds[n]) for n in range(1, 19))
 REVERSED = tuple((n, tuple(-v for v in lattice_speeds[n])) for n in range(1, 19))
-N_COPIES = sum(len(s) for s in crossing(MOVING))
+N_COPIES = sum(len(s) for face, s in enumerate(crossing(MOVING)) if face in (0, 1, 4))
 
 
 def opposite_of(number):
@@ -101,17 +101,13 @@
 
 def send_plan(sets, speeds, field, bufs, top, near):
     up_x, dn_x, up_y, dn_y, me_x, me_y = near
-    x_high, x_low, y_high, y_low, corners = sets
-    xhi, xlo, yhi, ylo, corner = bufs
+    x_high, x_low, _, _, corners = sets
+    xhi, xlo, _, _, corner = bufs
     plan = []
     for j, n in enumerate(x_high):
         plan.append((field(n).at[pl.ds(0, 8)], xhi.at[j], (dn_x, me_y)))
     for j, n in enumerate(x_low):
         plan.append((field(n).at[pl.ds(top, 8)], xlo.at[j], (up_x, me_y)))
-    for j, n in enumerate(y_high):
-        plan.append((field(n), yhi.at[j], (me_x, dn_y)))
-    for j, n in enumerate(y_low):
-        plan.append((field(n), ylo.at[j], (me_x, up_y)))
     for j, n in enumerate(corners):
         cx, cy, _ = speeds[n]
         rows_at = pl.ds(0, 8) if cx == 1 else pl.ds(top, 8)
@@ -153,7 +149,7 @@
     elif cx == -1:
         own = patch_x(own, xlo[x_low.index(n)])
     if cy != 0:
-        side = yhi[y_high.index(n)] if cy == 1 else ylo[y_low.index(n)]
+        side = yhi(n) if cy == 1 else ylo(n)
         if cx != 0:
             side = patch_x(side, corner[corners.index(n)])
         edge = 0 if cy == 1 else 127
@@ -170,12 +166,26 @@
     return own
 
 
+def pack_edge(fields, from_lane, rows):
+    lane = lax.broadcasted_iota(jnp.int32, (rows, 128), 1)
+    packed = jnp.zeros((rows, 128), jnp.float32)
+    for k, field in enumerate(fields):
+        moved = field if k == from_lane else pltpu.roll(field, (k - from_lane) % 128, 1)
+        packed = jnp.where(lane == k, moved, packed)
+    return packed
+
+
+def unpack_edge(packed_ref, k, to_lane):
+    packed = packed_ref[...]
+    return packed if k == to_lane else pltpu.roll(packed, (to_lane - k) % 128, 1)
+
+
 def drag_weight(number, flow, fluid):
     return (3.0 * lattice_weights[number]) * along_of(lattice_speeds[number], flow) * fluid
 
 
 def lbm_kernel(nx, ny, rows, scale, lam_hbm, vel_hbm, blk_hbm, out_ref, drag_ref,
-               lam_ref, vel_in, blk_ref, load_sem, vel_ref, fluid_ref, moved, state, hfield, xhi, xlo, yhi, ylo, corner, hxhi, hxlo, hyhi, hylo, hcorner,
+               lam_ref, vel_in, blk_ref, load_sem, vel_ref, fluid_ref, moved, state, hfield, xhi, xlo, yhi, ylo, corner, hxhi, hxlo, hcorner, ypack, ysend, yrecv,
                part, row_buf, col_buf, row_sum,
                ssem, rsem, hsend, hrecv, sum_send_a, sum_recv_a, sum_send_b, sum_recv_b):
     me_x = lax.axis_index("gx")
@@ -225,7 +235,15 @@
     h_sets = crossing(REVERSED)
     h_speeds = dict(REVERSED)
     lam_speeds = dict(MOVING)
-    h_bufs = (hxhi, hxlo, hyhi, hylo, hcorner)
+    n_hi = len(lam_sets[2])
+    n_lo = len(lam_sets[3])
+    h_bufs = (
+        hxhi,
+        hxlo,
+        lambda n: unpack_edge(yhi.at[0], n_hi + h_sets[2].index(n), 0),
+        lambda n: unpack_edge(ylo.at[0], n_lo + h_sets[3].index(n), 127),
+        hcorner,
+    )
     h_copies = None
     sent = []
     drag_acc = jnp.zeros((8, 128), jnp.float32)
@@ -233,12 +251,31 @@
     for step in range(STEPS):
         src = lam_ref if step == 0 else state
         origin = lam_hbm if step == 0 else state
-        bufs = (xhi.at[step], xlo.at[step], yhi.at[step], ylo.at[step], corner.at[step])
+        bufs = (
+            xhi.at[step],
+            xlo.at[step],
+            lambda n, s=step: unpack_edge(yhi.at[s], lam_sets[2].index(n), 0),
+            lambda n, s=step: unpack_edge(ylo.at[s], lam_sets[3].index(n), 127),
+            corner.at[step],
+        )
         plan = send_plan(lam_sets, lam_speeds, lambda n: origin.at[n], bufs, top, near)
         copies = start_copies(plan, ssem.at[step], rsem.at[step])
         if step == 0:
             h_plan = send_plan(h_sets, h_speeds, lambda n: hfield.at[n - 1], h_bufs, top, near)
             h_copies = start_copies(h_plan, hsend, hrecv)
+            loads[0].wait()
+        to_low = [src[n] for n in lam_sets[2]]
+        to_high = [src[n] for n in lam_sets[3]]
+        if step == 0:
+            to_low += [hfield[n - 1] for n in h_sets[2]]
+            to_high += [hfield[n - 1] for n in h_sets[3]]
+        ypack[step, 0] = pack_edge(to_low, 0, rows)
+        ypack[step, 1] = pack_edge(to_high, 127, rows)
+        copies += start_copies(
+            [(ypack.at[step, 0], yhi.at[step], (me_x, dn_y)), (ypack.at[step, 1], ylo.at[step], (me_x, up_y))],
+            ysend.at[step],
+            yrecv.at[step],
+        )
         if step == STEPS - 1:
             for copy in h_copies:
                 copy.wait_recv()
@@ -262,8 +299,6 @@
                 copy.start()
                 row_copies.append(copy)
             row_buf[me_y] = part[...]
-        if step == 0:
-            loads[0].wait()
         for copy in copies:
             copy.wait_recv()
         sent += copies
@@ -350,12 +385,19 @@
             pltpu.VMEM((q - 1, rows, rows_y), jnp.float32),
         ]
         + [
-            pltpu.VMEM((STEPS, len(s), rows if face >= 2 and face < 4 else 8, rows_y), jnp.float32)
-            for face, s in enumerate(crossing(MOVING))
+            pltpu.VMEM((STEPS, len(s), 8, rows_y), jnp.float32)
+            for face, s in enumerate(crossing(MOVING)) if face in (0, 1)
+        ]
+        + [pltpu.VMEM((STEPS, rows, rows_y), jnp.float32)] * 2
+        + [pltpu.VMEM((STEPS, len(crossing(MOVING)[4]), 8, rows_y), jnp.float32)]
+        + [
+            pltpu.VMEM((len(s), 8, rows_y), jnp.float32)
+            for face, s in enumerate(crossing(REVERSED)) if face in (0, 1, 4)
         ]
         + [
-            pltpu.VMEM((len(s), rows if face >= 2 and face < 4 else 8, rows_y), jnp.float32)
-            for face, s in enumerate(crossing(REVERSED))
+            pltpu.VMEM((STEPS, 2, rows, rows_y), jnp.float32),
+            pltpu.SemaphoreType.DMA((STEPS, 2)),
+            pltpu.SemaphoreType.DMA((STEPS, 2)),
         ]
         + [
             pltpu.VMEM((8, 128), jnp.float32),

time: 59.1 us -> 52.7 us (0.89)
  Pallas kernels: 54.6 us -> 48.3 us
    pallas_call x1, Pallas kernels: 54.6 us -> 48.3 us  [per_device(): pl.pallas_call(functools.partial(lbm_kernel, nx, ny, rows, scale), out_sh...]
where the time goes in v7:
time: 52.7 us; the launch traced here: 52.5 us
  Pallas kernels  48.3 us (92%)
  between operations  2.33 us (4%)
  local copies, waits for them, and re-layouts  1.96 us (4%)
    pallas_call x1, Pallas kernels, per_device(): pl.pallas_call(functools.partial(lbm_kernel, nx, ny, rows, scale), out_sh...  48.3 us
    unnamed x1, local copies, waits for them, and re-layouts  1.96 us

profile of v7, /device:TPU:1, one launch (start us, length us, event | category | flops | bytes accessed | tf_op | source)
XLA Modules:
  0.0 52.5 jit_solution(14259967751021078674)
XLA Ops:
  0.6 48.3 %shard_map.50 = (f32[19,64,128]{2,1,0:T(8,128)}, f32[1]{0:T(128)}) custom-call(f32[19,64,128]{2,1,0:T(8,128)} %bitcast.4, bf16[2,3,64,128]{3,2,1,0:T(8,128)(2,1)} %bitcast.7, s32[18,64,128]{2,1,0:T(8,128)} %bitcast.6), custom_call_target="tpu_custom_call" | custom-call | tf_op jit(solution)/shard_map/pallas_call | solution.py:368
  48.9 2.0 %copy.7 = f32[19,16,4,128]{3,2,1,0:T(4,128)} copy(f32[19,16,4,128]{3,2,1,0:T(4,128)} %bitcast.5) | data formatting | bytes 1245184

commit v8 on v7

--- a/solution.py
+++ b/solution.py
@@ -50,7 +50,7 @@
 
 MOVING = tuple((n, lattice_speeds[n]) for n in range(1, 19))
 REVERSED = tuple((n, tuple(-v for v in lattice_speeds[n])) for n in range(1, 19))
-N_COPIES = sum(len(s) for face, s in enumerate(crossing(MOVING)) if face in (0, 1, 4))
+N_COPIES = len(crossing(MOVING)[4])
 
 
 def opposite_of(number):
@@ -104,10 +104,6 @@
     x_high, x_low, _, _, corners = sets
     xhi, xlo, _, _, corner = bufs
     plan = []
-    for j, n in enumerate(x_high):
-        plan.append((field(n).at[pl.ds(0, 8)], xhi.at[j], (dn_x, me_y)))
-    for j, n in enumerate(x_low):
-        plan.append((field(n).at[pl.ds(top, 8)], xlo.at[j], (up_x, me_y)))
     for j, n in enumerate(corners):
         cx, cy, _ = speeds[n]
         rows_at = pl.ds(0, 8) if cx == 1 else pl.ds(top, 8)
@@ -145,9 +141,9 @@
         return jnp.concatenate([block[:top], tail], axis=0)
 
     if cx == 1:
-        own = patch_x(own, xhi[x_high.index(n)])
+        own = patch_x(own, xhi(n))
     elif cx == -1:
-        own = patch_x(own, xlo[x_low.index(n)])
+        own = patch_x(own, xlo(n))
     if cy != 0:
         side = yhi(n) if cy == 1 else ylo(n)
         if cx != 0:
@@ -175,6 +171,26 @@
     return packed
 
 
+def pack_rows(tiles, low_half):
+    row8 = lax.broadcasted_iota(jnp.int32, (8, 128), 0)
+    if len(tiles) % 2:
+        tiles = tiles + [jnp.zeros((8, 128), jnp.float32)]
+    packed = []
+    for a, b in zip(tiles[0::2], tiles[1::2]):
+        if low_half:
+            packed.append(jnp.where(row8 < 4, a, pltpu.roll(b, 4, 0)))
+        else:
+            packed.append(jnp.where(row8 >= 4, b, pltpu.roll(a, 4, 0)))
+    return jnp.concatenate(packed, axis=0)
+
+
+def unpack_rows(packed_ref, k, low_half):
+    tile = packed_ref[pl.ds(8 * (k // 2), 8)]
+    if (k % 2 == 0) == low_half:
+        return tile
+    return pltpu.roll(tile, 4, 0)
+
+
 def unpack_edge(packed_ref, k, to_lane):
     packed = packed_ref[...]
     return packed if k == to_lane else pltpu.roll(packed, (to_lane - k) % 128, 1)
@@ -185,7 +201,8 @@
 
 
 def lbm_kernel(nx, ny, rows, scale, lam_hbm, vel_hbm, blk_hbm, out_ref, drag_ref,
-               lam_ref, vel_in, blk_ref, load_sem, vel_ref, fluid_ref, moved, state, hfield, xhi, xlo, yhi, ylo, corner, hxhi, hxlo, hcorner, ypack, ysend, yrecv,
+               lam_ref, vel_in, blk_ref, load_sem, vel_ref, fluid_ref, moved, state, hfield, xhi, xlo, yhi, ylo, corner, hcorner, ypack, ysend, yrecv,
+               xpack_lo, xpack_hi, xsend, xrecv,
                part, row_buf, col_buf, row_sum,
                ssem, rsem, hsend, hrecv, sum_send_a, sum_recv_a, sum_send_b, sum_recv_b):
     me_x = lax.axis_index("gx")
@@ -237,9 +254,11 @@
     lam_speeds = dict(MOVING)
     n_hi = len(lam_sets[2])
     n_lo = len(lam_sets[3])
+    nx_hi = len(lam_sets[0])
+    nx_lo = len(lam_sets[1])
     h_bufs = (
-        hxhi,
-        hxlo,
+        lambda n: unpack_rows(xhi.at[0], nx_hi + h_sets[0].index(n), True),
+        lambda n: unpack_rows(xlo.at[0], nx_lo + h_sets[1].index(n), False),
         lambda n: unpack_edge(yhi.at[0], n_hi + h_sets[2].index(n), 0),
         lambda n: unpack_edge(ylo.at[0], n_lo + h_sets[3].index(n), 127),
         hcorner,
@@ -252,8 +271,8 @@
         src = lam_ref if step == 0 else state
         origin = lam_hbm if step == 0 else state
         bufs = (
-            xhi.at[step],
-            xlo.at[step],
+            lambda n, s=step: unpack_rows(xhi.at[s], lam_sets[0].index(n), True),
+            lambda n, s=step: unpack_rows(xlo.at[s], lam_sets[1].index(n), False),
             lambda n, s=step: unpack_edge(yhi.at[s], lam_sets[2].index(n), 0),
             lambda n, s=step: unpack_edge(ylo.at[s], lam_sets[3].index(n), 127),
             corner.at[step],
@@ -269,6 +288,23 @@
         if step == 0:
             to_low += [hfield[n - 1] for n in h_sets[2]]
             to_high += [hfield[n - 1] for n in h_sets[3]]
+        x_low_tiles = [src[n, 0:8] for n in lam_sets[0]]
+        x_high_tiles = [src[n, top:rows] for n in lam_sets[1]]
+        if step == 0:
+            x_low_tiles += [hfield[n - 1, 0:8] for n in h_sets[0]]
+            x_high_tiles += [hfield[n - 1, top:rows] for n in h_sets[1]]
+        count_lo = (len(x_low_tiles) + 1) // 2
+        count_hi = (len(x_high_tiles) + 1) // 2
+        xpack_lo[step, pl.ds(0, 8 * count_lo)] = pack_rows(x_low_tiles, True)
+        xpack_hi[step, pl.ds(0, 8 * count_hi)] = pack_rows(x_high_tiles, False)
+        copies += start_copies(
+            [
+                (xpack_lo.at[step, pl.ds(0, 8 * count_lo)], xhi.at[step, pl.ds(0, 8 * count_lo)], (dn_x, me_y)),
+                (xpack_hi.at[step, pl.ds(0, 8 * count_hi)], xlo.at[step, pl.ds(0, 8 * count_hi)], (up_x, me_y)),
+            ],
+            xsend.at[step],
+            xrecv.at[step],
+        )
         ypack[step, 0] = pack_edge(to_low, 0, rows)
         ypack[step, 1] = pack_edge(to_high, 127, rows)
         copies += start_copies(
@@ -365,6 +401,9 @@
     cell_count = rows_x * nx * rows_y * ny * levels
     scale = drag_factor / math.sqrt(cell_count)
     vmem = pl.BlockSpec(memory_space=pltpu.VMEM)
+    x_tiles = max(
+        (len(crossing(MOVING)[face]) + len(crossing(REVERSED)[face]) + 1) // 2 for face in (0, 1)
+    )
     state, drag = pl.pallas_call(
         functools.partial(lbm_kernel, nx, ny, rows, scale),
         out_shape=(
@@ -384,18 +423,16 @@
             pltpu.VMEM((q, rows, rows_y), jnp.float32),
             pltpu.VMEM((q - 1, rows, rows_y), jnp.float32),
         ]
-        + [
-            pltpu.VMEM((STEPS, len(s), 8, rows_y), jnp.float32)
-            for face, s in enumerate(crossing(MOVING)) if face in (0, 1)
-        ]
+        + [pltpu.VMEM((STEPS, 8 * x_tiles, rows_y), jnp.float32)] * 2
         + [pltpu.VMEM((STEPS, rows, rows_y), jnp.float32)] * 2
         + [pltpu.VMEM((STEPS, len(crossing(MOVING)[4]), 8, rows_y), jnp.float32)]
-        + [
-            pltpu.VMEM((len(s), 8, rows_y), jnp.float32)
-            for face, s in enumerate(crossing(REVERSED)) if face in (0, 1, 4)
-        ]
+        + [pltpu.VMEM((len(crossing(REVERSED)[4]), 8, rows_y), jnp.float32)]
         + [
             pltpu.VMEM((STEPS, 2, rows, rows_y), jnp.float32),
+            pltpu.SemaphoreType.DMA((STEPS, 2)),
+            pltpu.SemaphoreType.DMA((STEPS, 2)),
+            pltpu.VMEM((STEPS, 8 * x_tiles, rows_y), jnp.float32),
+            pltpu.VMEM((STEPS, 8 * x_tiles, rows_y), jnp.float32),
             pltpu.SemaphoreType.DMA((STEPS, 2)),
             pltpu.SemaphoreType.DMA((STEPS, 2)),
         ]

time: 52.7 us -> 52 us (0.987)
  Pallas kernels: 48.3 us -> 47.5 us
    pallas_call x1, Pallas kernels: 48.3 us -> 47.5 us  [per_device(): pl.pallas_call(functools.partial(lbm_kernel, nx, ny, rows, scale), out_sh...]
where the time goes in v8:
time: 52 us; the launch traced here: 51.7 us
  Pallas kernels  47.5 us (91%)
  between operations  2.33 us (4%)
  local copies, waits for them, and re-layouts  1.96 us (4%)
    pallas_call x1, Pallas kernels, per_device(): pl.pallas_call(functools.partial(lbm_kernel, nx, ny, rows, scale), out_sh...  47.5 us
    unnamed x1, local copies, waits for them, and re-layouts  1.96 us

profile of v8, /device:TPU:1, one launch (start us, length us, event | category | flops | bytes accessed | tf_op | source)
XLA Modules:
  0.0 51.7 jit_solution(781716935686338717)
XLA Ops:
  0.6 47.5 %shard_map.50 = (f32[19,64,128]{2,1,0:T(8,128)}, f32[1]{0:T(128)}) custom-call(f32[19,64,128]{2,1,0:T(8,128)} %bitcast.4, bf16[2,3,64,128]{3,2,1,0:T(8,128)(2,1)} %bitcast.7, s32[18,64,128]{2,1,0:T(8,128)} %bitcast.6), custom_call_target="tpu_custom_call" | custom-call | tf_op jit(solution)/shard_map/pallas_call | solution.py:407
  48.1 2.0 %copy.7 = f32[19,16,4,128]{3,2,1,0:T(4,128)} copy(f32[19,16,4,128]{3,2,1,0:T(4,128)} %bitcast.5) | data formatting | bytes 1245184

commit v9 on v8

--- a/solution.py
+++ b/solution.py
@@ -221,12 +221,21 @@
     for load in loads:
         load.start()
 
+    half = nx // 2
+    my_half = me_x // half
+    in_half = lax.rem(me_x, half)
+    a_peers = []
+    for dz in range(2):
+        for k in range(ny):
+            if dz == 0 and k == 0:
+                continue
+            a_peers.append((k + dz * ny, (in_half + lax.rem(my_half + dz, 2) * half, lax.rem(me_y + k, ny))))
+    b_peers = [(k, (my_half * half + lax.rem(in_half + k, half), me_y)) for k in range(1, half)]
+
     barrier = pltpu.get_barrier_semaphore()
-    for k in range(1, ny):
-        pl.semaphore_signal(barrier, inc=1, device_id=(me_x, lax.rem(me_y + k, ny)), device_id_type=MESH)
-    for k in range(1, nx):
-        pl.semaphore_signal(barrier, inc=1, device_id=(lax.rem(me_x + k, nx), me_y), device_id_type=MESH)
-    for dev in ((up_x, up_y), (up_x, dn_y), (dn_x, up_y), (dn_x, dn_y)):
+    for _, dev in a_peers + b_peers:
+        pl.semaphore_signal(barrier, inc=1, device_id=dev, device_id_type=MESH)
+    for dev in ((up_x, up_y), (up_x, dn_y), (dn_x, up_y), (dn_x, dn_y), (up_x, me_y), (dn_x, me_y)):
         pl.semaphore_signal(barrier, inc=1, device_id=dev, device_id_type=MESH)
 
     loads[1].wait()
@@ -246,7 +255,7 @@
         weight = drag_weight(number, last_flow, fluid_all)
         hfield[number - 1] = jnp.where(blk_ref[number - 1] == 1, 0.0, weight)
 
-    pl.semaphore_wait(barrier, nx + ny + 2)
+    pl.semaphore_wait(barrier, len(a_peers) + len(b_peers) + 6)
 
     lam_sets = crossing(MOVING)
     h_sets = crossing(REVERSED)
@@ -326,15 +335,15 @@
                 bounced = jnp.where(blk_ref[number - 1] == 1, src[opposite_of(number)] + 2.0 * cx, 0.0)
                 total = total + jnp.sum((weight * bounced).reshape(rows // 8, 8, 128), axis=0)
             part[...] = jnp.broadcast_to(jnp.sum(total), (8, 128))
+            a_slot = my_half * ny + me_y
             row_copies = []
-            for k in range(1, ny):
+            for k, dev in a_peers:
                 copy = pltpu.make_async_remote_copy(
-                    src_ref=part, dst_ref=row_buf.at[me_y], send_sem=sum_send_a.at[k],
-                    recv_sem=sum_recv_a.at[k], device_id=(me_x, lax.rem(me_y + k, ny)),
-                    device_id_type=MESH)
+                    src_ref=part, dst_ref=row_buf.at[a_slot], send_sem=sum_send_a.at[k],
+                    recv_sem=sum_recv_a.at[k], device_id=dev, device_id_type=MESH)
                 copy.start()
                 row_copies.append(copy)
-            row_buf[me_y] = part[...]
+            row_buf[a_slot] = part[...]
         for copy in copies:
             copy.wait_recv()
         sent += copies
@@ -350,18 +359,17 @@
                 copy.wait_recv()
             sent += row_copies
             total = row_buf[0]
-            for j in range(1, ny):
+            for j in range(1, 2 * ny):
                 total = total + row_buf[j]
             row_sum[...] = total
             col_copies = []
-            for k in range(1, nx):
+            for k, dev in b_peers:
                 copy = pltpu.make_async_remote_copy(
-                    src_ref=row_sum, dst_ref=col_buf.at[me_x], send_sem=sum_send_b.at[k],
-                    recv_sem=sum_recv_b.at[k], device_id=(lax.rem(me_x + k, nx), me_y),
-                    device_id_type=MESH)
+                    src_ref=row_sum, dst_ref=col_buf.at[in_half], send_sem=sum_send_b.at[k],
+                    recv_sem=sum_recv_b.at[k], device_id=dev, device_id_type=MESH)
                 copy.start()
                 col_copies.append(copy)
-            col_buf[me_x] = total
+            col_buf[in_half] = total
 
         dest = out_ref if step == STEPS - 1 else state
 
@@ -383,7 +391,7 @@
         copy.wait_recv()
     sent += col_copies
     total = col_buf[0]
-    for j in range(1, nx):
+    for j in range(1, nx // 2):
         total = total + col_buf[j]
     drag_ref[0] = -scale * total[0, 0]
     for copy in sent:
@@ -438,17 +446,17 @@
         ]
         + [
             pltpu.VMEM((8, 128), jnp.float32),
-            pltpu.VMEM((ny, 8, 128), jnp.float32),
-            pltpu.VMEM((nx, 8, 128), jnp.float32),
+            pltpu.VMEM((2 * ny, 8, 128), jnp.float32),
+            pltpu.VMEM((nx // 2, 8, 128), jnp.float32),
             pltpu.VMEM((8, 128), jnp.float32),
             pltpu.SemaphoreType.DMA((STEPS, N_COPIES)),
             pltpu.SemaphoreType.DMA((STEPS, N_COPIES)),
             pltpu.SemaphoreType.DMA((N_COPIES,)),
             pltpu.SemaphoreType.DMA((N_COPIES,)),
-            pltpu.SemaphoreType.DMA((ny,)),
-            pltpu.SemaphoreType.DMA((ny,)),
-            pltpu.SemaphoreType.DMA((nx,)),
-            pltpu.SemaphoreType.DMA((nx,)),
+            pltpu.SemaphoreType.DMA((2 * ny,)),
+            pltpu.SemaphoreType.DMA((2 * ny,)),
+            pltpu.SemaphoreType.DMA((nx // 2,)),
+            pltpu.SemaphoreType.DMA((nx // 2,)),
         ],
         compiler_params=pltpu.CompilerParams(collective_id=0, has_side_effects=True),
     )(lam, flow, blocked)

time: 52 us -> 56.4 us (1.085)
  Pallas kernels: 47.5 us -> 51.9 us
    pallas_call x1, Pallas kernels: 47.5 us -> 51.9 us  [per_device(): pl.pallas_call(functools.partial(lbm_kernel, nx, ny, rows, scale), out_sh...]
where the time goes in v9:
time: 56.4 us; the launch traced here: 56.2 us
  Pallas kernels  51.9 us (92%)
  between operations  2.33 us (4%)
  local copies, waits for them, and re-layouts  1.96 us (3%)
    pallas_call x1, Pallas kernels, per_device(): pl.pallas_call(functools.partial(lbm_kernel, nx, ny, rows, scale), out_sh...  51.9 us
    unnamed x1, local copies, waits for them, and re-layouts  1.96 us

profile of v9, /device:TPU:1, one launch (start us, length us, event | category | flops | bytes accessed | tf_op | source)
XLA Modules:
  0.0 56.2 jit_solution(10987033784343457587)
XLA Ops:
  0.6 51.9 %shard_map.50 = (f32[19,64,128]{2,1,0:T(8,128)}, f32[1]{0:T(128)}) custom-call(f32[19,64,128]{2,1,0:T(8,128)} %bitcast.4, bf16[2,3,64,128]{3,2,1,0:T(8,128)(2,1)} %bitcast.7, s32[18,64,128]{2,1,0:T(8,128)} %bitcast.6), custom_call_target="tpu_custom_call" | custom-call | tf_op jit(solution)/shard_map/pallas_call | solution.py:415
  52.5 2.0 %copy.7 = f32[19,16,4,128]{3,2,1,0:T(4,128)} copy(f32[19,16,4,128]{3,2,1,0:T(4,128)} %bitcast.5) | data formatting | bytes 1245184

commit v10 on v8

--- a/solution.py
+++ b/solution.py
@@ -335,17 +335,6 @@
                 copy.start()
                 row_copies.append(copy)
             row_buf[me_y] = part[...]
-        for copy in copies:
-            copy.wait_recv()
-        sent += copies
-
-        moved[0] = src[0]
-        for number in range(1, 19):
-            source = shifted(src[number], lam_speeds[number], number, lam_sets, bufs, rows)
-            bounced = src[opposite_of(number)] + 2.0 * lam_speeds[number][0]
-            moved[number] = jnp.where(blk_ref[number - 1] == 1, bounced, source)
-
-        if step == STEPS - 1:
             for copy in row_copies:
                 copy.wait_recv()
             sent += row_copies
@@ -362,6 +351,16 @@
                 copy.start()
                 col_copies.append(copy)
             col_buf[me_x] = total
+        for copy in copies:
+            copy.wait_recv()
+        sent += copies
+
+        moved[0] = src[0]
+        for number in range(1, 19):
+            source = shifted(src[number], lam_speeds[number], number, lam_sets, bufs, rows)
+            bounced = src[opposite_of(number)] + 2.0 * lam_speeds[number][0]
+            moved[number] = jnp.where(blk_ref[number - 1] == 1, bounced, source)
+
 
         dest = out_ref if step == STEPS - 1 else state
 

time: 52 us -> 52 us (level)
  no operation moved by 1% of the time
where the time goes in v10:
time: 52 us; the launch traced here: 51.7 us
  Pallas kernels  47.5 us (91%)
  between operations  2.33 us (4%)
  local copies, waits for them, and re-layouts  1.96 us (4%)
    pallas_call x1, Pallas kernels, per_device(): pl.pallas_call(functools.partial(lbm_kernel, nx, ny, rows, scale), out_sh...  47.5 us
    unnamed x1, local copies, waits for them, and re-layouts  1.96 us

profile of v10, /device:TPU:1, one launch (start us, length us, event | category | flops | bytes accessed | tf_op | source)
XLA Modules:
  0.0 51.7 jit_solution(13214834343083440744)
XLA Ops:
  0.6 47.5 %shard_map.50 = (f32[19,64,128]{2,1,0:T(8,128)}, f32[1]{0:T(128)}) custom-call(f32[19,64,128]{2,1,0:T(8,128)} %bitcast.4, bf16[2,3,64,128]{3,2,1,0:T(8,128)(2,1)} %bitcast.7, s32[18,64,128]{2,1,0:T(8,128)} %bitcast.6), custom_call_target="tpu_custom_call" | custom-call | tf_op jit(solution)/shard_map/pallas_call | solution.py:406
  48.1 2.0 %copy.7 = f32[19,16,4,128]{3,2,1,0:T(4,128)} copy(f32[19,16,4,128]{3,2,1,0:T(4,128)} %bitcast.5) | data formatting | bytes 1245184

commit v11 on v10

--- a/solution.py
+++ b/solution.py
@@ -9,6 +9,7 @@
 from jax.sharding import PartitionSpec as P
 
 MESH = pl.DeviceIdType.MESH
+SPAN_X = 4
 TILE = 4
 STEPS = 2
 
@@ -200,11 +201,34 @@
     return (3.0 * lattice_weights[number]) * along_of(lattice_speeds[number], flow) * fluid
 
 
+def start_gather(value_ref, buf, slot, peers, send_sems, recv_sems):
+    copies = []
+    for k, dev in peers:
+        copy = pltpu.make_async_remote_copy(
+            src_ref=value_ref, dst_ref=buf.at[slot], send_sem=send_sems.at[k],
+            recv_sem=recv_sems.at[k], device_id=dev, device_id_type=MESH)
+        copy.start()
+        copies.append(copy)
+    return copies
+
+
+def gather_sum(value_ref, buf, slot, peers, send_sems, recv_sems, sent):
+    copies = start_gather(value_ref, buf, slot, peers, send_sems, recv_sems)
+    buf[slot] = value_ref[...]
+    for copy in copies:
+        copy.wait_recv()
+    sent += copies
+    total = buf[0]
+    for j in range(1, len(peers) + 1):
+        total = total + buf[j]
+    return total
+
+
 def lbm_kernel(nx, ny, rows, scale, lam_hbm, vel_hbm, blk_hbm, out_ref, drag_ref,
                lam_ref, vel_in, blk_ref, load_sem, vel_ref, fluid_ref, moved, state, hfield, xhi, xlo, yhi, ylo, corner, hcorner, ypack, ysend, yrecv,
                xpack_lo, xpack_hi, xsend, xrecv,
-               part, row_buf, col_buf, row_sum,
-               ssem, rsem, hsend, hrecv, sum_send_a, sum_recv_a, sum_send_b, sum_recv_b):
+               part, g1_buf, g2_buf, g3_buf, g1_sum, g2_sum,
+               ssem, rsem, hsend, hrecv, g1_send, g1_recv, g2_send, g2_recv, g3_send, g3_recv):
     me_x = lax.axis_index("gx")
     me_y = lax.axis_index("gy")
     up_x = lax.rem(me_x + 1, nx)
@@ -221,12 +245,22 @@
     for load in loads:
         load.start()
 
+    b1, b2 = nx // 2, SPAN_X
+    n3 = 2 * (ny // b2)
+    slot1 = lax.rem(me_x, b1)
+    slot2 = lax.rem(me_y, b2)
+    slot3 = (me_x // b1) * (ny // b2) + me_y // b2
+    peers1 = [(k, ((me_x // b1) * b1 + lax.rem(slot1 + k, b1), me_y)) for k in range(1, b1)]
+    peers2 = [(k, (me_x, (me_y // b2) * b2 + lax.rem(slot2 + k, b2))) for k in range(1, b2)]
+    peers3 = []
+    for k in range(1, n3):
+        t = lax.rem(slot3 + k, n3)
+        peers3.append((k, ((t // (ny // b2)) * b1 + slot1, lax.rem(t, ny // b2) * b2 + slot2)))
+
     barrier = pltpu.get_barrier_semaphore()
-    for k in range(1, ny):
-        pl.semaphore_signal(barrier, inc=1, device_id=(me_x, lax.rem(me_y + k, ny)), device_id_type=MESH)
-    for k in range(1, nx):
-        pl.semaphore_signal(barrier, inc=1, device_id=(lax.rem(me_x + k, nx), me_y), device_id_type=MESH)
-    for dev in ((up_x, up_y), (up_x, dn_y), (dn_x, up_y), (dn_x, dn_y)):
+    for _, dev in peers1 + peers2 + peers3:
+        pl.semaphore_signal(barrier, inc=1, device_id=dev, device_id_type=MESH)
+    for dev in ((up_x, up_y), (up_x, dn_y), (dn_x, up_y), (dn_x, dn_y), (up_x, me_y), (dn_x, me_y), (me_x, up_y), (me_x, dn_y)):
         pl.semaphore_signal(barrier, inc=1, device_id=dev, device_id_type=MESH)
 
     loads[1].wait()
@@ -246,7 +280,7 @@
         weight = drag_weight(number, last_flow, fluid_all)
         hfield[number - 1] = jnp.where(blk_ref[number - 1] == 1, 0.0, weight)
 
-    pl.semaphore_wait(barrier, nx + ny + 2)
+    pl.semaphore_wait(barrier, len(peers1) + len(peers2) + len(peers3) + 8)
 
     lam_sets = crossing(MOVING)
     h_sets = crossing(REVERSED)
@@ -326,31 +360,12 @@
                 bounced = jnp.where(blk_ref[number - 1] == 1, src[opposite_of(number)] + 2.0 * cx, 0.0)
                 total = total + jnp.sum((weight * bounced).reshape(rows // 8, 8, 128), axis=0)
             part[...] = jnp.broadcast_to(jnp.sum(total), (8, 128))
-            row_copies = []
-            for k in range(1, ny):
-                copy = pltpu.make_async_remote_copy(
-                    src_ref=part, dst_ref=row_buf.at[me_y], send_sem=sum_send_a.at[k],
-                    recv_sem=sum_recv_a.at[k], device_id=(me_x, lax.rem(me_y + k, ny)),
-                    device_id_type=MESH)
-                copy.start()
-                row_copies.append(copy)
-            row_buf[me_y] = part[...]
-            for copy in row_copies:
-                copy.wait_recv()
-            sent += row_copies
-            total = row_buf[0]
-            for j in range(1, ny):
-                total = total + row_buf[j]
-            row_sum[...] = total
-            col_copies = []
-            for k in range(1, nx):
-                copy = pltpu.make_async_remote_copy(
-                    src_ref=row_sum, dst_ref=col_buf.at[me_x], send_sem=sum_send_b.at[k],
-                    recv_sem=sum_recv_b.at[k], device_id=(lax.rem(me_x + k, nx), me_y),
-                    device_id_type=MESH)
-                copy.start()
-                col_copies.append(copy)
-            col_buf[me_x] = total
+            total = gather_sum(part, g1_buf, slot1, peers1, g1_send, g1_recv, sent)
+            g1_sum[...] = total
+            total = gather_sum(g1_sum, g2_buf, slot2, peers2, g2_send, g2_recv, sent)
+            g2_sum[...] = total
+            g3_copies = start_gather(g2_sum, g3_buf, slot3, peers3, g3_send, g3_recv)
+            g3_buf[slot3] = total
         for copy in copies:
             copy.wait_recv()
         sent += copies
@@ -378,12 +393,12 @@
         else:
             lax.fori_loop(0, rows // 8, chunk, drag_acc)
 
-    for copy in col_copies:
+    for copy in g3_copies:
         copy.wait_recv()
-    sent += col_copies
-    total = col_buf[0]
-    for j in range(1, nx):
-        total = total + col_buf[j]
+    sent += g3_copies
+    total = g3_buf[0]
+    for j in range(1, n3):
+        total = total + g3_buf[j]
     drag_ref[0] = -scale * total[0, 0]
     for copy in sent:
         copy.wait_send()
@@ -437,17 +452,21 @@
         ]
         + [
             pltpu.VMEM((8, 128), jnp.float32),
-            pltpu.VMEM((ny, 8, 128), jnp.float32),
-            pltpu.VMEM((nx, 8, 128), jnp.float32),
+            pltpu.VMEM((nx // 2, 8, 128), jnp.float32),
+            pltpu.VMEM((SPAN_X, 8, 128), jnp.float32),
+            pltpu.VMEM((2 * ny // SPAN_X, 8, 128), jnp.float32),
+            pltpu.VMEM((8, 128), jnp.float32),
             pltpu.VMEM((8, 128), jnp.float32),
             pltpu.SemaphoreType.DMA((STEPS, N_COPIES)),
             pltpu.SemaphoreType.DMA((STEPS, N_COPIES)),
             pltpu.SemaphoreType.DMA((N_COPIES,)),
             pltpu.SemaphoreType.DMA((N_COPIES,)),
-            pltpu.SemaphoreType.DMA((ny,)),
-            pltpu.SemaphoreType.DMA((ny,)),
-            pltpu.SemaphoreType.DMA((nx,)),
-            pltpu.SemaphoreType.DMA((nx,)),
+            pltpu.SemaphoreType.DMA((nx // 2,)),
+            pltpu.SemaphoreType.DMA((nx // 2,)),
+            pltpu.SemaphoreType.DMA((SPAN_X,)),
+            pltpu.SemaphoreType.DMA((SPAN_X,)),
+            pltpu.SemaphoreType.DMA((2 * ny // SPAN_X,)),
+            pltpu.SemaphoreType.DMA((2 * ny // SPAN_X,)),
         ],
         compiler_params=pltpu.CompilerParams(collective_id=0, has_side_effects=True),
     )(lam, flow, blocked)

time: 52 us -> 49.6 us (0.954)
  Pallas kernels: 47.5 us -> 45.1 us
    pallas_call x1, Pallas kernels: 47.5 us -> 45.1 us  [per_device(): pl.pallas_call(functools.partial(lbm_kernel, nx, ny, rows, scale), out_sh...]
where the time goes in v11:
time: 49.6 us; the launch traced here: 49.4 us
  Pallas kernels  45.1 us (91%)
  between operations  2.33 us (5%)
  local copies, waits for them, and re-layouts  1.96 us (4%)
    pallas_call x1, Pallas kernels, per_device(): pl.pallas_call(functools.partial(lbm_kernel, nx, ny, rows, scale), out_sh...  45.1 us
    unnamed x1, local copies, waits for them, and re-layouts  1.96 us

profile of v11, /device:TPU:1, one launch (start us, length us, event | category | flops | bytes accessed | tf_op | source)
XLA Modules:
  0.0 49.4 jit_solution(16498855698360436751)
XLA Ops:
  0.6 45.1 %shard_map.50 = (f32[19,64,128]{2,1,0:T(8,128)}, f32[1]{0:T(128)}) custom-call(f32[19,64,128]{2,1,0:T(8,128)} %bitcast.4, bf16[2,3,64,128]{3,2,1,0:T(8,128)(2,1)} %bitcast.7, s32[18,64,128]{2,1,0:T(8,128)} %bitcast.6), custom_call_target="tpu_custom_call" | custom-call | tf_op jit(solution)/shard_map/pallas_call | solution.py:421
  45.8 2.0 %copy.7 = f32[19,16,4,128]{3,2,1,0:T(4,128)} copy(f32[19,16,4,128]{3,2,1,0:T(4,128)} %bitcast.5) | data formatting | bytes 1245184

commit v12 on v11

--- a/solution.py
+++ b/solution.py
@@ -227,8 +227,8 @@
 def lbm_kernel(nx, ny, rows, scale, lam_hbm, vel_hbm, blk_hbm, out_ref, drag_ref,
                lam_ref, vel_in, blk_ref, load_sem, vel_ref, fluid_ref, moved, state, hfield, xhi, xlo, yhi, ylo, corner, hcorner, ypack, ysend, yrecv,
                xpack_lo, xpack_hi, xsend, xrecv,
-               part, g1_buf, g2_buf, g3_buf, g1_sum, g2_sum,
-               ssem, rsem, hsend, hrecv, g1_send, g1_recv, g2_send, g2_recv, g3_send, g3_recv):
+               part, g1_buf, g2_buf, g3_buf, g4_buf, g1_sum, g2_sum, g3_sum,
+               ssem, rsem, hsend, hrecv, g1_send, g1_recv, g2_send, g2_recv, g3_send, g3_recv, g4_send, g4_recv):
     me_x = lax.axis_index("gx")
     me_y = lax.axis_index("gy")
     up_x = lax.rem(me_x + 1, nx)
@@ -252,13 +252,20 @@
     slot3 = (me_x // b1) * (ny // b2) + me_y // b2
     peers1 = [(k, ((me_x // b1) * b1 + lax.rem(slot1 + k, b1), me_y)) for k in range(1, b1)]
     peers2 = [(k, (me_x, (me_y // b2) * b2 + lax.rem(slot2 + k, b2))) for k in range(1, b2)]
-    peers3 = []
-    for k in range(1, n3):
-        t = lax.rem(slot3 + k, n3)
-        peers3.append((k, ((t // (ny // b2)) * b1 + slot1, lax.rem(t, ny // b2) * b2 + slot2)))
+    near_z = min(4, n3)
+    far_z = n3 // near_z
+
+    def z_device(t):
+        return ((t // (ny // b2)) * b1 + slot1, lax.rem(t, ny // b2) * b2 + slot2)
+
+    slot3_all = slot3
+    slot3 = lax.rem(slot3_all, near_z)
+    slot4 = slot3_all // near_z
+    peers3 = [(k, z_device(slot4 * near_z + lax.rem(slot3 + k, near_z))) for k in range(1, near_z)]
+    peers4 = [(k, z_device(lax.rem(slot4 + k, far_z) * near_z + slot3)) for k in range(1, far_z)]
 
     barrier = pltpu.get_barrier_semaphore()
-    for _, dev in peers1 + peers2 + peers3:
+    for _, dev in peers1 + peers2 + peers3 + peers4:
         pl.semaphore_signal(barrier, inc=1, device_id=dev, device_id_type=MESH)
     for dev in ((up_x, up_y), (up_x, dn_y), (dn_x, up_y), (dn_x, dn_y), (up_x, me_y), (dn_x, me_y), (me_x, up_y), (me_x, dn_y)):
         pl.semaphore_signal(barrier, inc=1, device_id=dev, device_id_type=MESH)
@@ -280,7 +287,7 @@
         weight = drag_weight(number, last_flow, fluid_all)
         hfield[number - 1] = jnp.where(blk_ref[number - 1] == 1, 0.0, weight)
 
-    pl.semaphore_wait(barrier, len(peers1) + len(peers2) + len(peers3) + 8)
+    pl.semaphore_wait(barrier, len(peers1) + len(peers2) + len(peers3) + len(peers4) + 8)
 
     lam_sets = crossing(MOVING)
     h_sets = crossing(REVERSED)
@@ -364,8 +371,10 @@
             g1_sum[...] = total
             total = gather_sum(g1_sum, g2_buf, slot2, peers2, g2_send, g2_recv, sent)
             g2_sum[...] = total
-            g3_copies = start_gather(g2_sum, g3_buf, slot3, peers3, g3_send, g3_recv)
-            g3_buf[slot3] = total
+            total = gather_sum(g2_sum, g3_buf, slot3, peers3, g3_send, g3_recv, sent)
+            g3_sum[...] = total
+            g4_copies = start_gather(g3_sum, g4_buf, slot4, peers4, g4_send, g4_recv)
+            g4_buf[slot4] = total
         for copy in copies:
             copy.wait_recv()
         sent += copies
@@ -393,12 +402,12 @@
         else:
             lax.fori_loop(0, rows // 8, chunk, drag_acc)
 
-    for copy in g3_copies:
+    for copy in g4_copies:
         copy.wait_recv()
-    sent += g3_copies
-    total = g3_buf[0]
-    for j in range(1, n3):
-        total = total + g3_buf[j]
+    sent += g4_copies
+    total = g4_buf[0]
+    for j in range(1, far_z):
+        total = total + g4_buf[j]
     drag_ref[0] = -scale * total[0, 0]
     for copy in sent:
         copy.wait_send()
@@ -415,6 +424,7 @@
     cell_count = rows_x * nx * rows_y * ny * levels
     scale = drag_factor / math.sqrt(cell_count)
     vmem = pl.BlockSpec(memory_space=pltpu.VMEM)
+    NEAR_Z = min(4, 2 * ny // SPAN_X)
     x_tiles = max(
         (len(crossing(MOVING)[face]) + len(crossing(REVERSED)[face]) + 1) // 2 for face in (0, 1)
     )
@@ -454,7 +464,9 @@
             pltpu.VMEM((8, 128), jnp.float32),
             pltpu.VMEM((nx // 2, 8, 128), jnp.float32),
             pltpu.VMEM((SPAN_X, 8, 128), jnp.float32),
-            pltpu.VMEM((2 * ny // SPAN_X, 8, 128), jnp.float32),
+            pltpu.VMEM((NEAR_Z, 8, 128), jnp.float32),
+            pltpu.VMEM((2 * ny // SPAN_X // NEAR_Z, 8, 128), jnp.float32),
+            pltpu.VMEM((8, 128), jnp.float32),
             pltpu.VMEM((8, 128), jnp.float32),
             pltpu.VMEM((8, 128), jnp.float32),
             pltpu.SemaphoreType.DMA((STEPS, N_COPIES)),
@@ -465,8 +477,10 @@
             pltpu.SemaphoreType.DMA((nx // 2,)),
             pltpu.SemaphoreType.DMA((SPAN_X,)),
             pltpu.SemaphoreType.DMA((SPAN_X,)),
-            pltpu.SemaphoreType.DMA((2 * ny // SPAN_X,)),
-            pltpu.SemaphoreType.DMA((2 * ny // SPAN_X,)),
+            pltpu.SemaphoreType.DMA((NEAR_Z,)),
+            pltpu.SemaphoreType.DMA((NEAR_Z,)),
+            pltpu.SemaphoreType.DMA((2 * ny // SPAN_X // NEAR_Z,)),
+            pltpu.SemaphoreType.DMA((2 * ny // SPAN_X // NEAR_Z,)),
         ],
         compiler_params=pltpu.CompilerParams(collective_id=0, has_side_effects=True),
     )(lam, flow, blocked)

time: 49.6 us -> 50.6 us (1.020); the launches traced: 49.4 us -> 49.6 us
  no operation moved by 1% of the time
where the time goes in v12:
time: 50.6 us; the launch traced here: 49.6 us
  Pallas kernels  45.3 us (90%)
  between operations  2.33 us (5%)
  local copies, waits for them, and re-layouts  1.96 us (4%)
    pallas_call x1, Pallas kernels, per_device(): pl.pallas_call(functools.partial(lbm_kernel, nx, ny, rows, scale), out_sh...  45.3 us
    unnamed x1, local copies, waits for them, and re-layouts  1.96 us

profile of v12, /device:TPU:1, one launch (start us, length us, event | category | flops | bytes accessed | tf_op | source)
XLA Modules:
  0.0 49.6 jit_solution(7133754768290938108)
XLA Ops:
  0.6 45.3 %shard_map.50 = (f32[19,64,128]{2,1,0:T(8,128)}, f32[1]{0:T(128)}) custom-call(f32[19,64,128]{2,1,0:T(8,128)} %bitcast.4, bf16[2,3,64,128]{3,2,1,0:T(8,128)(2,1)} %bitcast.7, s32[18,64,128]{2,1,0:T(8,128)} %bitcast.6), custom_call_target="tpu_custom_call" | custom-call | tf_op jit(solution)/shard_map/pallas_call | solution.py:431
  45.9 2.0 %copy.7 = f32[19,16,4,128]{3,2,1,0:T(4,128)} copy(f32[19,16,4,128]{3,2,1,0:T(4,128)} %bitcast.5) | data formatting | bytes 1245184

commit v13 on v11

--- a/solution.py
+++ b/solution.py
@@ -250,15 +250,18 @@
     slot1 = lax.rem(me_x, b1)
     slot2 = lax.rem(me_y, b2)
     slot3 = (me_x // b1) * (ny // b2) + me_y // b2
-    peers1 = [(k, ((me_x // b1) * b1 + lax.rem(slot1 + k, b1), me_y)) for k in range(1, b1)]
-    peers2 = [(k, (me_x, (me_y // b2) * b2 + lax.rem(slot2 + k, b2))) for k in range(1, b2)]
+    slot12 = slot1 * b2 + slot2
+    peers12 = []
+    for k in range(1, b1 * b2):
+        t = lax.rem(slot12 + k, b1 * b2)
+        peers12.append((k, ((me_x // b1) * b1 + t // b2, (me_y // b2) * b2 + lax.rem(t, b2))))
     peers3 = []
     for k in range(1, n3):
         t = lax.rem(slot3 + k, n3)
         peers3.append((k, ((t // (ny // b2)) * b1 + slot1, lax.rem(t, ny // b2) * b2 + slot2)))
 
     barrier = pltpu.get_barrier_semaphore()
-    for _, dev in peers1 + peers2 + peers3:
+    for _, dev in peers12 + peers3:
         pl.semaphore_signal(barrier, inc=1, device_id=dev, device_id_type=MESH)
     for dev in ((up_x, up_y), (up_x, dn_y), (dn_x, up_y), (dn_x, dn_y), (up_x, me_y), (dn_x, me_y), (me_x, up_y), (me_x, dn_y)):
         pl.semaphore_signal(barrier, inc=1, device_id=dev, device_id_type=MESH)
@@ -280,7 +283,7 @@
         weight = drag_weight(number, last_flow, fluid_all)
         hfield[number - 1] = jnp.where(blk_ref[number - 1] == 1, 0.0, weight)
 
-    pl.semaphore_wait(barrier, len(peers1) + len(peers2) + len(peers3) + 8)
+    pl.semaphore_wait(barrier, len(peers12) + len(peers3) + 8)
 
     lam_sets = crossing(MOVING)
     h_sets = crossing(REVERSED)
@@ -360,9 +363,7 @@
                 bounced = jnp.where(blk_ref[number - 1] == 1, src[opposite_of(number)] + 2.0 * cx, 0.0)
                 total = total + jnp.sum((weight * bounced).reshape(rows // 8, 8, 128), axis=0)
             part[...] = jnp.broadcast_to(jnp.sum(total), (8, 128))
-            total = gather_sum(part, g1_buf, slot1, peers1, g1_send, g1_recv, sent)
-            g1_sum[...] = total
-            total = gather_sum(g1_sum, g2_buf, slot2, peers2, g2_send, g2_recv, sent)
+            total = gather_sum(part, g1_buf, slot12, peers12, g1_send, g1_recv, sent)
             g2_sum[...] = total
             g3_copies = start_gather(g2_sum, g3_buf, slot3, peers3, g3_send, g3_recv)
             g3_buf[slot3] = total
@@ -452,7 +453,7 @@
         ]
         + [
             pltpu.VMEM((8, 128), jnp.float32),
-            pltpu.VMEM((nx // 2, 8, 128), jnp.float32),
+            pltpu.VMEM((nx // 2 * SPAN_X, 8, 128), jnp.float32),
             pltpu.VMEM((SPAN_X, 8, 128), jnp.float32),
             pltpu.VMEM((2 * ny // SPAN_X, 8, 128), jnp.float32),
             pltpu.VMEM((8, 128), jnp.float32),
@@ -461,8 +462,8 @@
             pltpu.SemaphoreType.DMA((STEPS, N_COPIES)),
             pltpu.SemaphoreType.DMA((N_COPIES,)),
             pltpu.SemaphoreType.DMA((N_COPIES,)),
-            pltpu.SemaphoreType.DMA((nx // 2,)),
-            pltpu.SemaphoreType.DMA((nx // 2,)),
+            pltpu.SemaphoreType.DMA((nx // 2 * SPAN_X,)),
+            pltpu.SemaphoreType.DMA((nx // 2 * SPAN_X,)),
             pltpu.SemaphoreType.DMA((SPAN_X,)),
             pltpu.SemaphoreType.DMA((SPAN_X,)),
             pltpu.SemaphoreType.DMA((2 * ny // SPAN_X,)),

time: 49.6 us -> 49.1 us (0.990)
  Pallas kernels: 45.1 us -> 44.6 us
    pallas_call x1, Pallas kernels: 45.1 us -> 44.6 us  [per_device(): pl.pallas_call(functools.partial(lbm_kernel, nx, ny, rows, scale), out_sh...]
where the time goes in v13:
time: 49.1 us; the launch traced here: 48.9 us
  Pallas kernels  44.6 us (91%)
  between operations  2.33 us (5%)
  local copies, waits for them, and re-layouts  1.96 us (4%)
    pallas_call x1, Pallas kernels, per_device(): pl.pallas_call(functools.partial(lbm_kernel, nx, ny, rows, scale), out_sh...  44.6 us
    unnamed x1, local copies, waits for them, and re-layouts  1.96 us

profile of v13, /device:TPU:1, one launch (start us, length us, event | category | flops | bytes accessed | tf_op | source)
XLA Modules:
  0.0 48.9 jit_solution(2018119511179736303)
XLA Ops:
  0.6 44.6 %shard_map.50 = (f32[19,64,128]{2,1,0:T(8,128)}, f32[1]{0:T(128)}) custom-call(f32[19,64,128]{2,1,0:T(8,128)} %bitcast.4, bf16[2,3,64,128]{3,2,1,0:T(8,128)(2,1)} %bitcast.7, s32[18,64,128]{2,1,0:T(8,128)} %bitcast.6), custom_call_target="tpu_custom_call" | custom-call | tf_op jit(solution)/shard_map/pallas_call | solution.py:422
  45.2 2.0 %copy.7 = f32[19,16,4,128]{3,2,1,0:T(4,128)} copy(f32[19,16,4,128]{3,2,1,0:T(4,128)} %bitcast.5) | data formatting | bytes 1245184

commit v14 on v13

--- a/solution.py
+++ b/solution.py
@@ -363,10 +363,8 @@
                 bounced = jnp.where(blk_ref[number - 1] == 1, src[opposite_of(number)] + 2.0 * cx, 0.0)
                 total = total + jnp.sum((weight * bounced).reshape(rows // 8, 8, 128), axis=0)
             part[...] = jnp.broadcast_to(jnp.sum(total), (8, 128))
-            total = gather_sum(part, g1_buf, slot12, peers12, g1_send, g1_recv, sent)
-            g2_sum[...] = total
-            g3_copies = start_gather(g2_sum, g3_buf, slot3, peers3, g3_send, g3_recv)
-            g3_buf[slot3] = total
+            g1_copies = start_gather(part, g1_buf, slot12, peers12, g1_send, g1_recv)
+            g1_buf[slot12] = part[...]
         for copy in copies:
             copy.wait_recv()
         sent += copies
@@ -377,6 +375,17 @@
             bounced = src[opposite_of(number)] + 2.0 * lam_speeds[number][0]
             moved[number] = jnp.where(blk_ref[number - 1] == 1, bounced, source)
 
+
+        if step == STEPS - 1:
+            for copy in g1_copies:
+                copy.wait_recv()
+            sent += g1_copies
+            total = g1_buf[0]
+            for j in range(1, len(peers12) + 1):
+                total = total + g1_buf[j]
+            g2_sum[...] = total
+            g3_copies = start_gather(g2_sum, g3_buf, slot3, peers3, g3_send, g3_recv)
+            g3_buf[slot3] = total
 
         dest = out_ref if step == STEPS - 1 else state
 

time: 49.1 us -> 49 us (level)
  no operation moved by 1% of the time
where the time goes in v14:
time: 49 us; the launch traced here: 48.8 us
  Pallas kernels  44.5 us (91%)
  between operations  2.33 us (5%)
  local copies, waits for them, and re-layouts  1.96 us (4%)
    pallas_call x1, Pallas kernels, per_device(): pl.pallas_call(functools.partial(lbm_kernel, nx, ny, rows, scale), out_sh...  44.5 us
    unnamed x1, local copies, waits for them, and re-layouts  1.96 us

profile of v14, /device:TPU:1, one launch (start us, length us, event | category | flops | bytes accessed | tf_op | source)
XLA Modules:
  0.0 48.8 jit_solution(11838726060077302989)
XLA Ops:
  0.6 44.5 %shard_map.50 = (f32[19,64,128]{2,1,0:T(8,128)}, f32[1]{0:T(128)}) custom-call(f32[19,64,128]{2,1,0:T(8,128)} %bitcast.4, bf16[2,3,64,128]{3,2,1,0:T(8,128)(2,1)} %bitcast.7, s32[18,64,128]{2,1,0:T(8,128)} %bitcast.6), custom_call_target="tpu_custom_call" | custom-call | tf_op jit(solution)/shard_map/pallas_call | solution.py:431
  45.1 2.0 %copy.7 = f32[19,16,4,128]{3,2,1,0:T(4,128)} copy(f32[19,16,4,128]{3,2,1,0:T(4,128)} %bitcast.5) | data formatting | bytes 1245184

commit v15 on v14

--- a/solution.py
+++ b/solution.py
@@ -105,7 +105,7 @@
     x_high, x_low, _, _, corners = sets
     xhi, xlo, _, _, corner = bufs
     plan = []
-    for j, n in enumerate(corners):
+    for j, n in enumerate(()):
         cx, cy, _ = speeds[n]
         rows_at = pl.ds(0, 8) if cx == 1 else pl.ds(top, 8)
         dev_x = dn_x if cx == 1 else up_x
@@ -148,7 +148,7 @@
     if cy != 0:
         side = yhi(n) if cy == 1 else ylo(n)
         if cx != 0:
-            side = patch_x(side, corner[corners.index(n)])
+            side = patch_x(side, corner(n))
         edge = 0 if cy == 1 else 127
         own = jnp.where(lane == edge, side, own)
     shift = 4 * cx + cz
@@ -298,7 +298,7 @@
         lambda n: unpack_rows(xlo.at[0], nx_lo + h_sets[1].index(n), False),
         lambda n: unpack_edge(yhi.at[0], n_hi + h_sets[2].index(n), 0),
         lambda n: unpack_edge(ylo.at[0], n_lo + h_sets[3].index(n), 127),
-        hcorner,
+        lambda n: unpack_rows(corner.at[0], 2 * lam_sets[4].index(opposite_of(n)) + 1, h_speeds[n][0] == 1),
     )
     h_copies = None
     sent = []
@@ -312,7 +312,7 @@
             lambda n, s=step: unpack_rows(xlo.at[s], lam_sets[1].index(n), False),
             lambda n, s=step: unpack_edge(yhi.at[s], lam_sets[2].index(n), 0),
             lambda n, s=step: unpack_edge(ylo.at[s], lam_sets[3].index(n), 127),
-            corner.at[step],
+            lambda n, s=step: unpack_rows(corner.at[s], 2 * lam_sets[4].index(n), lam_speeds[n][0] == 1),
         )
         plan = send_plan(lam_sets, lam_speeds, lambda n: origin.at[n], bufs, top, near)
         copies = start_copies(plan, ssem.at[step], rsem.at[step])
@@ -320,6 +320,17 @@
             h_plan = send_plan(h_sets, h_speeds, lambda n: hfield.at[n - 1], h_bufs, top, near)
             h_copies = start_copies(h_plan, hsend, hrecv)
             loads[0].wait()
+        corner_plan = []
+        for d, n in enumerate(lam_sets[4]):
+            cx, cy, _ = lam_speeds[n]
+            rows_at = slice(0, 8) if cx == 1 else slice(top, rows)
+            tiles = [src[n, rows_at]]
+            if step == 0:
+                tiles.append(hfield[opposite_of(n) - 1, rows_at])
+            hcorner[step, pl.ds(8 * d, 8)] = pack_rows(tiles, cx == 1)
+            dev = (dn_x if cx == 1 else up_x, dn_y if cy == 1 else up_y)
+            corner_plan.append((hcorner.at[step, pl.ds(8 * d, 8)], corner.at[step, pl.ds(8 * d, 8)], dev))
+        copies += start_copies(corner_plan, ssem.at[step], rsem.at[step])
         to_low = [src[n] for n in lam_sets[2]]
         to_high = [src[n] for n in lam_sets[3]]
         if step == 0:
@@ -449,8 +460,7 @@
         ]
         + [pltpu.VMEM((STEPS, 8 * x_tiles, rows_y), jnp.float32)] * 2
         + [pltpu.VMEM((STEPS, rows, rows_y), jnp.float32)] * 2
-        + [pltpu.VMEM((STEPS, len(crossing(MOVING)[4]), 8, rows_y), jnp.float32)]
-        + [pltpu.VMEM((len(crossing(REVERSED)[4]), 8, rows_y), jnp.float32)]
+        + [pltpu.VMEM((STEPS, 8 * len(crossing(MOVING)[4]), rows_y), jnp.float32)] * 2
         + [
             pltpu.VMEM((STEPS, 2, rows, rows_y), jnp.float32),
             pltpu.SemaphoreType.DMA((STEPS, 2)),

time: 49 us -> 48.3 us (0.986)
  Pallas kernels: 44.5 us -> 43.6 us
    pallas_call x1, Pallas kernels: 44.5 us -> 43.6 us  [per_device(): pl.pallas_call(functools.partial(lbm_kernel, nx, ny, rows, scale), out_sh...]
where the time goes in v15:
time: 48.3 us; the launch traced here: 47.9 us
  Pallas kernels  43.6 us (90%)
  between operations  2.33 us (5%)
  local copies, waits for them, and re-layouts  1.96 us (4%)
    pallas_call x1, Pallas kernels, per_device(): pl.pallas_call(functools.partial(lbm_kernel, nx, ny, rows, scale), out_sh...  43.6 us
    unnamed x1, local copies, waits for them, and re-layouts  1.96 us

profile of v15, /device:TPU:1, one launch (start us, length us, event | category | flops | bytes accessed | tf_op | source)
XLA Modules:
  0.0 47.9 jit_solution(5572239019501552808)
XLA Ops:
  0.6 43.6 %shard_map.50 = (f32[19,64,128]{2,1,0:T(8,128)}, f32[1]{0:T(128)}) custom-call(f32[19,64,128]{2,1,0:T(8,128)} %bitcast.4, bf16[2,3,64,128]{3,2,1,0:T(8,128)(2,1)} %bitcast.7, s32[18,64,128]{2,1,0:T(8,128)} %bitcast.6), custom_call_target="tpu_custom_call" | custom-call | tf_op jit(solution)/shard_map/pallas_call | solution.py:442
  44.2 2.0 %copy.7 = f32[19,16,4,128]{3,2,1,0:T(4,128)} copy(f32[19,16,4,128]{3,2,1,0:T(4,128)} %bitcast.5) | data formatting | bytes 1245184

commit v16 on v15

--- a/solution.py
+++ b/solution.py
@@ -376,12 +376,17 @@
             part[...] = jnp.broadcast_to(jnp.sum(total), (8, 128))
             g1_copies = start_gather(part, g1_buf, slot12, peers12, g1_send, g1_recv)
             g1_buf[slot12] = part[...]
+        local = tuple(n for n in range(1, 19) if lam_speeds[n][0] == 0 and lam_speeds[n][1] == 0)
+        moved[0] = src[0]
+        for number in local:
+            source = shifted(src[number], lam_speeds[number], number, lam_sets, bufs, rows)
+            bounced = src[opposite_of(number)] + 2.0 * lam_speeds[number][0]
+            moved[number] = jnp.where(blk_ref[number - 1] == 1, bounced, source)
         for copy in copies:
             copy.wait_recv()
         sent += copies
 
-        moved[0] = src[0]
-        for number in range(1, 19):
+        for number in (n for n in range(1, 19) if n not in local):
             source = shifted(src[number], lam_speeds[number], number, lam_sets, bufs, rows)
             bounced = src[opposite_of(number)] + 2.0 * lam_speeds[number][0]
             moved[number] = jnp.where(blk_ref[number - 1] == 1, bounced, source)

time: 48.3 us -> 48.3 us (level)
  no operation moved by 1% of the time
where the time goes in v16:
time: 48.3 us; the launch traced here: 47.9 us
  Pallas kernels  43.6 us (90%)
  between operations  2.33 us (5%)
  local copies, waits for them, and re-layouts  1.96 us (4%)
    pallas_call x1, Pallas kernels, per_device(): pl.pallas_call(functools.partial(lbm_kernel, nx, ny, rows, scale), out_sh...  43.6 us
    unnamed x1, local copies, waits for them, and re-layouts  1.96 us

profile of v16, /device:TPU:1, one launch (start us, length us, event | category | flops | bytes accessed | tf_op | source)
XLA Modules:
  0.0 47.9 jit_solution(14933117316644858297)
XLA Ops:
  0.6 43.6 %shard_map.50 = (f32[19,64,128]{2,1,0:T(8,128)}, f32[1]{0:T(128)}) custom-call(f32[19,64,128]{2,1,0:T(8,128)} %bitcast.4, bf16[2,3,64,128]{3,2,1,0:T(8,128)(2,1)} %bitcast.7, s32[18,64,128]{2,1,0:T(8,128)} %bitcast.6), custom_call_target="tpu_custom_call" | custom-call | tf_op jit(solution)/shard_map/pallas_call | solution.py:447
  44.2 2.0 %copy.7 = f32[19,16,4,128]{3,2,1,0:T(4,128)} copy(f32[19,16,4,128]{3,2,1,0:T(4,128)} %bitcast.5) | data formatting | bytes 1245184

commit v17 on v16

--- a/solution.py
+++ b/solution.py
@@ -382,14 +382,22 @@
             source = shifted(src[number], lam_speeds[number], number, lam_sets, bufs, rows)
             bounced = src[opposite_of(number)] + 2.0 * lam_speeds[number][0]
             moved[number] = jnp.where(blk_ref[number - 1] == 1, bounced, source)
-        for copy in copies:
-            copy.wait_recv()
+        n_corner = len(lam_sets[4])
+        waves = (
+            (copies[n_corner + 2:], lambda c: c[0] == 0 and c[1] != 0),
+            (copies[n_corner:n_corner + 2], lambda c: c[0] != 0 and c[1] == 0),
+            (copies[:n_corner], lambda c: c[0] != 0 and c[1] != 0),
+        )
+        for wave, wanted in waves:
+            for copy in wave:
+                copy.wait_recv()
+            for number in range(1, 19):
+                if number in local or not wanted(lam_speeds[number]):
+                    continue
+                source = shifted(src[number], lam_speeds[number], number, lam_sets, bufs, rows)
+                bounced = src[opposite_of(number)] + 2.0 * lam_speeds[number][0]
+                moved[number] = jnp.where(blk_ref[number - 1] == 1, bounced, source)
         sent += copies
-
-        for number in (n for n in range(1, 19) if n not in local):
-            source = shifted(src[number], lam_speeds[number], number, lam_sets, bufs, rows)
-            bounced = src[opposite_of(number)] + 2.0 * lam_speeds[number][0]
-            moved[number] = jnp.where(blk_ref[number - 1] == 1, bounced, source)
 
 
         if step == STEPS - 1:

time: 48.3 us -> 48.1 us (level)
  no operation moved by 1% of the time
where the time goes in v17:
time: 48.1 us; the launch traced here: 47.7 us
  Pallas kernels  43.4 us (90%)
  between operations  2.33 us (5%)
  local copies, waits for them, and re-layouts  1.96 us (4%)
    pallas_call x1, Pallas kernels, per_device(): pl.pallas_call(functools.partial(lbm_kernel, nx, ny, rows, scale), out_sh...  43.4 us
    unnamed x1, local copies, waits for them, and re-layouts  1.96 us

profile of v17, /device:TPU:1, one launch (start us, length us, event | category | flops | bytes accessed | tf_op | source)
XLA Modules:
  0.0 47.7 jit_solution(4597055112434286885)
XLA Ops:
  0.6 43.4 %shard_map.50 = (f32[19,64,128]{2,1,0:T(8,128)}, f32[1]{0:T(128)}) custom-call(f32[19,64,128]{2,1,0:T(8,128)} %bitcast.4, bf16[2,3,64,128]{3,2,1,0:T(8,128)(2,1)} %bitcast.7, s32[18,64,128]{2,1,0:T(8,128)} %bitcast.6), custom_call_target="tpu_custom_call" | custom-call | tf_op jit(solution)/shard_map/pallas_call | solution.py:455
  44.0 2.0 %copy.7 = f32[19,16,4,128]{3,2,1,0:T(4,128)} copy(f32[19,16,4,128]{3,2,1,0:T(4,128)} %bitcast.5) | data formatting | bytes 1245184
